TPU v7x, 32 devices: a whole 2x2x4 slice. The times are simulated.
32 devices in a mesh: dp: 4 (over x, core), ctx: 2 (over y), tensor: 4 (over z).
Axes of the slice: x: 2, y: 2, z: 4, core: 2. Of those that a mesh axis runs over, the one named last changes fastest.
Arguments:
- tokens: bfloat16 [4, 1024, 768], P('dp', 'ctx'), may hold values from -24 to 24
- lengths: int32 [4], P('dp'), may hold values from 128 to 1024, as said below
- cotangent: bfloat16 [4, 1024, 768], P('dp', 'ctx'), may hold values from -6 to 6
- qkv_weight: bfloat16 [3, 768, 768], P(None, 'dp', 'tensor'), may hold values from -0.21875 to 0.21875
- query_bias: float32 [768], P('tensor'), may hold values from -3 to 3
- value_bias: float32 [768], P('tensor'), may hold values from -0.18 to 0.18
- proj_weight: bfloat16 [768, 768], P('tensor', 'dp'), may hold values from -6 to 6
- proj_bias: float32 [768], replicated, may hold values from -2 to 2
- first_gain: float32 [768], replicated, may hold values from 0.1 to 1.9
- first_shift: float32 [768], replicated, may hold values from -2 to 2
- up_weight: bfloat16 [768, 3072], P('dp', 'tensor'), may hold values from -0.21875 to 0.21875
- up_bias: float32 [3072], P('tensor'), may hold values from -2 to 2
- down_weight: bfloat16 [3072, 768], P('tensor', 'dp'), may hold values from -0.109375 to 0.109375
- down_bias: float32 [768], replicated, may hold values from -2 to 2
- second_gain: float32 [768], replicated, may hold values from 0.1 to 1.9
- second_shift: float32 [768], replicated, may hold values from -2 to 2
Outputs:
- output: bfloat16 [4, 1024, 768], P('dp', 'ctx')
- grad_tokens: float32 [4, 1024, 768], P('dp', 'ctx')
- grad_qkv: float32 [3, 768, 768], P(None, 'dp', 'tensor')
- grad_query_bias: float32 [768], P('tensor')
- grad_value_bias: float32 [768], P('tensor')
- grad_proj: float32 [768, 768], P('tensor', 'dp')
- grad_proj_bias: float32 [768], replicated
- grad_first_gain: float32 [768], replicated
- grad_first_shift: float32 [768], replicated
- grad_up: float32 [768, 3072], P('dp', 'tensor')
- grad_up_bias: float32 [3072], P('tensor')
- grad_down: float32 [3072, 768], P('tensor', 'dp')
- grad_down_bias: float32 [768], replicated
- grad_second_gain: float32 [768], replicated
- grad_second_shift: float32 [768], replicated
Inputs may be any that keep to these rules, and one draw needn't show every extreme that they name: `lengths`: positions at or beyond a sequence's length are padding; they are still computed, but no position attends to them.
All inputs are finite; a program needn't handle non-finite values.
Results may differ from a plain program's by a relative error of at most 0.013.
The roundings to bfloat16 on the way count: a program that leaves them out, or rounds other values in their place, can miss the bound.
Values may be sent and summed in bfloat16 or wider, within the bound.
A program may use at most 128 MiB of HBM per device.

v0:
```python
import math

import jax
import jax.numpy as jnp
from jax import lax
from jax.sharding import PartitionSpec as P

HD = 64


EPSILON = 1e-05
NEGATIVE = -1e30
ROOT_HALF = 0.7071067811865476
ROOT_TWO_PI = 2.5066282746310002


def layer_norm(hidden_in, norm_gain, norm_shift):
    centred = hidden_in - jnp.mean(hidden_in, axis=-1, keepdims=True)
    inverse = lax.rsqrt(jnp.mean(centred * centred, axis=-1, keepdims=True) + EPSILON)
    normed = centred * inverse
    return (normed * norm_gain + norm_shift, normed, inverse)


def norm_back(upstream, normed, inverse, norm_gain):
    scaled = upstream * norm_gain
    return inverse * (
        scaled
        - jnp.mean(scaled, axis=-1, keepdims=True)
        - normed * jnp.mean(scaled * normed, axis=-1, keepdims=True)
    )


def gelu_value(pre_act):
    return 0.5 * pre_act * (1.0 + jax.scipy.special.erf(pre_act * ROOT_HALF))


def gelu_slope(pre_act):
    return (
        0.5 * (1.0 + jax.scipy.special.erf(pre_act * ROOT_HALF))
        + pre_act * jnp.exp(-0.5 * pre_act * pre_act) / ROOT_TWO_PI
    )


def attend_piece(running, pieces, queries, length, score_scale):
    key_piece, value_piece = pieces
    piece_rows = key_piece.shape[0]
    block_width = math.gcd(piece_rows, 512)
    block_count = piece_rows // block_width
    heads_here = key_piece.shape[1]
    key_blocks = key_piece.reshape(block_count, block_width, heads_here, HD)
    value_blocks = value_piece.reshape(block_count, block_width, heads_here, HD)

    def one_block(carried, block_item):
        run_max, run_total, run_acc = carried
        key_block, value_block, block_index = block_item
        positions = block_index * block_width + jnp.arange(block_width, dtype=jnp.int32)
        key_mask = (positions < length)[None, None, :]
        scores = (
            jnp.einsum("qhe,khe->hqk", queries, key_block, preferred_element_type=jnp.float32)
            * score_scale
        )
        scores = jnp.where(key_mask, scores, NEGATIVE)
        new_max = jnp.maximum(run_max, jnp.max(scores, axis=-1))
        rescale = jnp.exp(run_max - new_max)
        weights_now = jnp.where(key_mask, jnp.exp(scores - new_max[..., None]), 0.0)
        run_total = run_total * rescale + jnp.sum(weights_now, axis=-1)
        run_acc = run_acc * rescale.T[..., None] + jnp.einsum(
            "hqk,khe->qhe",
            weights_now.astype(jnp.bfloat16),
            value_block,
            preferred_element_type=jnp.float32,
        )
        return ((new_max, run_total, run_acc), None)

    block_numbers = jnp.arange(block_count, dtype=jnp.int32)
    carried, unused = lax.scan(one_block, running, (key_blocks, value_blocks, block_numbers))
    return carried


def per_device(
    tokens,
    lengths,
    cotangent,
    qkv_weight,
    query_bias,
    value_bias,
    proj_weight,
    proj_bias,
    first_gain,
    first_shift,
    up_weight,
    up_bias,
    down_weight,
    down_bias,
    second_gain,
    second_shift,
):
    wide_qkv, wide_proj, wide_up, wide_down = (
        lax.all_gather(qkv_weight, "dp", axis=1, tiled=True),
        lax.all_gather(proj_weight, "dp", axis=1, tiled=True),
        lax.all_gather(up_weight, "dp", axis=0, tiled=True),
        lax.all_gather(down_weight, "dp", axis=1, tiled=True),
    )
    rows_in = tokens[0]
    length = lengths[0]
    row_count = rows_in.shape[0]
    local_width = wide_qkv.shape[2]
    heads_here = local_width // HD
    score_scale = 1.0 / math.sqrt(HD)
    projected = jnp.einsum("td,ide->ite", rows_in, wide_qkv, preferred_element_type=jnp.float32)
    queries = (projected[0] + query_bias).astype(jnp.bfloat16).reshape(row_count, heads_here, HD)
    key_rows = projected[1].astype(jnp.bfloat16).reshape(row_count, heads_here, HD)
    value_rows = (projected[2] + value_bias).astype(jnp.bfloat16).reshape(row_count, heads_here, HD)
    initial = (
        jnp.full((heads_here, row_count), NEGATIVE, jnp.float32),
        jnp.zeros((heads_here, row_count), jnp.float32),
        jnp.zeros((row_count, heads_here, HD), jnp.float32),
    )
    run_max, run_total, run_acc = attend_piece(
        initial,
        (
            lax.all_gather(key_rows, "ctx", axis=0, tiled=True),
            lax.all_gather(value_rows, "ctx", axis=0, tiled=True),
        ),
        queries,
        length,
        score_scale,
    )
    attended = run_acc / run_total.T[..., None]
    log_total = run_max + jnp.log(run_total)
    attended_low = attended.reshape(row_count, local_width).astype(jnp.bfloat16)
    attn_part = jnp.dot(attended_low, wide_proj, preferred_element_type=jnp.float32)
    first_sum = rows_in.astype(jnp.float32) + lax.psum(attn_part, "tensor") + proj_bias
    first_out, first_normed, first_inverse = layer_norm(first_sum, first_gain, first_shift)
    first_low = first_out.astype(jnp.bfloat16)
    pre_act = jnp.dot(first_low, wide_up, preferred_element_type=jnp.float32) + up_bias
    hidden = gelu_value(pre_act).astype(jnp.bfloat16)
    down_part = jnp.dot(hidden, wide_down, preferred_element_type=jnp.float32)
    second_sum = first_out + lax.psum(down_part, "tensor") + down_bias
    result, second_normed, second_inverse = layer_norm(second_sum, second_gain, second_shift)
    output = result.astype(jnp.bfloat16)[None]
    upstream = cotangent[0].astype(jnp.float32)
    grad_second_shift = jnp.sum(upstream, axis=0)
    grad_second_gain = jnp.sum(upstream * second_normed, axis=0)
    d_second = norm_back(upstream, second_normed, second_inverse, second_gain)
    grad_down_bias = jnp.sum(d_second, axis=0)
    d_second_low = d_second.astype(jnp.bfloat16)
    grad_down = jnp.einsum("tf,td->fd", hidden, d_second_low, preferred_element_type=jnp.float32)
    d_hidden = jnp.einsum("td,fd->tf", d_second_low, wide_down, preferred_element_type=jnp.float32)
    d_pre = d_hidden * gelu_slope(pre_act)
    grad_up_bias = jnp.sum(d_pre, axis=0)
    d_pre_low = d_pre.astype(jnp.bfloat16)
    grad_up = jnp.einsum("td,tf->df", first_low, d_pre_low, preferred_element_type=jnp.float32)
    first_part = jnp.einsum("tf,df->td", d_pre_low, wide_up, preferred_element_type=jnp.float32)
    d_first = lax.psum(first_part, "tensor") + d_second
    grad_first_shift = jnp.sum(d_first, axis=0)
    grad_first_gain = jnp.sum(d_first * first_normed, axis=0)
    d_attn = norm_back(d_first, first_normed, first_inverse, first_gain)
    grad_proj_bias = jnp.sum(d_attn, axis=0)
    d_attn_low = d_attn.astype(jnp.bfloat16)
    grad_proj = jnp.einsum(
        "te,td->ed", attended_low, d_attn_low, preferred_element_type=jnp.float32
    )
    d_heads = jnp.einsum("td,ed->te", d_attn_low, wide_proj, preferred_element_type=jnp.float32)
    d_heads = d_heads.astype(jnp.bfloat16).reshape(row_count, heads_here, HD)
    row_delta = jnp.sum(d_heads.astype(jnp.float32) * attended, axis=-1).T
    key_back, value_back = (
        lax.all_gather(key_rows, "ctx", axis=0, tiled=True),
        lax.all_gather(value_rows, "ctx", axis=0, tiled=True),
    )
    seq_rows = key_back.shape[0]
    block_width = math.gcd(seq_rows, 512)
    block_count = seq_rows // block_width

    def back_block(d_query, block_item):
        key_block, value_block, block_index = block_item
        positions = block_index * block_width + jnp.arange(block_width, dtype=jnp.int32)
        key_mask = (positions < length)[None, None, :]
        scores = (
            jnp.einsum("qhe,khe->hqk", queries, key_block, preferred_element_type=jnp.float32)
            * score_scale
        )
        scores = jnp.where(key_mask, scores, NEGATIVE)
        probabilities = jnp.where(key_mask, jnp.exp(scores - log_total[..., None]), 0.0)
        probs_low = probabilities.astype(jnp.bfloat16)
        value_grad = jnp.einsum(
            "hqk,qhe->khe", probs_low, d_heads, preferred_element_type=jnp.float32
        )
        d_probs = jnp.einsum(
            "qhe,khe->hqk", d_heads, value_block, preferred_element_type=jnp.float32
        )
        d_scores = (probabilities * (d_probs - row_delta[..., None])).astype(jnp.bfloat16)
        d_query = (
            d_query
            + jnp.einsum("hqk,khe->qhe", d_scores, key_block, preferred_element_type=jnp.float32)
            * score_scale
        )
        key_grad = (
            jnp.einsum("hqk,qhe->khe", d_scores, queries, preferred_element_type=jnp.float32)
            * score_scale
        )
        return (d_query, (key_grad, value_grad))

    block_items = (
        key_back.reshape(block_count, block_width, heads_here, HD),
        value_back.reshape(block_count, block_width, heads_here, HD),
        jnp.arange(block_count, dtype=jnp.int32),
    )
    d_query, (key_grads, value_grads) = lax.scan(
        back_block, jnp.zeros((row_count, heads_here, HD), jnp.float32), block_items
    )
    key_grads = key_grads.reshape(seq_rows, heads_here, HD)
    value_grads = value_grads.reshape(seq_rows, heads_here, HD)
    own_keys, own_values = (
        lax.psum_scatter(key_grads, "ctx", scatter_dimension=0, tiled=True),
        lax.psum_scatter(value_grads, "ctx", scatter_dimension=0, tiled=True),
    )
    query_flat = d_query.reshape(row_count, local_width)
    key_flat = own_keys.reshape(row_count, local_width)
    value_flat = own_values.reshape(row_count, local_width)
    grad_query_bias = jnp.sum(query_flat, axis=0)
    grad_value_bias = jnp.sum(value_flat, axis=0)
    d_stack = jnp.stack(
        [
            query_flat.astype(jnp.bfloat16),
            key_flat.astype(jnp.bfloat16),
            value_flat.astype(jnp.bfloat16),
        ]
    )
    grad_qkv = jnp.einsum("td,ite->ide", rows_in, d_stack, preferred_element_type=jnp.float32)
    input_part = jnp.einsum("ite,ide->td", d_stack, wide_qkv, preferred_element_type=jnp.float32)
    grad_tokens = (d_attn + lax.psum(input_part, "tensor"))[None]
    local_grads = (grad_qkv, grad_proj, grad_up, grad_down)
    grad_pieces = (
        lax.psum_scatter(local_grads[0], ("dp", "ctx"), scatter_dimension=1, tiled=True),
        lax.psum_scatter(local_grads[1], ("dp", "ctx"), scatter_dimension=1, tiled=True),
        lax.psum_scatter(local_grads[2], ("dp", "ctx"), scatter_dimension=0, tiled=True),
        lax.psum_scatter(local_grads[3], ("dp", "ctx"), scatter_dimension=1, tiled=True),
    )
    owned_grads = (
        lax.all_gather(grad_pieces[0], "ctx", axis=1, tiled=True),
        lax.all_gather(grad_pieces[1], "ctx", axis=1, tiled=True),
        lax.all_gather(grad_pieces[2], "ctx", axis=0, tiled=True),
        lax.all_gather(grad_pieces[3], "ctx", axis=1, tiled=True),
    )
    vector_grads = lax.psum(
        (
            grad_query_bias,
            grad_value_bias,
            grad_proj_bias,
            grad_first_gain,
            grad_first_shift,
            grad_up_bias,
            grad_down_bias,
            grad_second_gain,
            grad_second_shift,
        ),
        ("dp", "ctx"),
    )
    return (
        output,
        grad_tokens,
        owned_grads[0],
        vector_grads[0],
        vector_grads[1],
        owned_grads[1],
        vector_grads[2],
        vector_grads[3],
        vector_grads[4],
        owned_grads[2],
        vector_grads[5],
        owned_grads[3],
        vector_grads[6],
        vector_grads[7],
        vector_grads[8],
    )


def solution(mesh):
    placed = (
        P("dp", "ctx", None),
        P("dp"),
        P("dp", "ctx", None),
        P(None, "dp", "tensor"),
        P("tensor"),
        P("tensor"),
        P("tensor", "dp"),
        P(),
        P(),
        P(),
        P("dp", "tensor"),
        P("tensor"),
        P("tensor", "dp"),
        P(),
        P(),
        P(),
    )
    return jax.shard_map(
        per_device,
        mesh=mesh,
        in_specs=placed,
        out_specs=(
            P("dp", "ctx", None),
            P("dp", "ctx", None),
            P(None, "dp", "tensor"),
            P("tensor"),
            P("tensor"),
            P("tensor", "dp"),
            P(),
            P(),
            P(),
            P("dp", "tensor"),
            P("tensor"),
            P("tensor", "dp"),
            P(),
            P(),
            P(),
        ),
        check_vma=False,
    )
```

profile of v0, /device:TPU:0, one launch (start us, length us, event | category | flops | bytes accessed | tf_op | source)
XLA Modules:
  0.0 575.8 jit_solution(4283684153634687425)
XLA Ops:
  9.4 14.3 %all_gather.32 = bf16[3,768,192]{2,0,1:T(4,128)(2,1)S(1)} all-gather(bf16[3,192,192]{2,0,1:T(4,128)(2,1)S(1)} %copy.46), channel_id=1, replica_groups=mesh['dp'=4,'ctx'=2,'tensor'=4] {'dp'}, dimensions={1}, use_global_device_ids=true | all-gather | bytes 1105920 | tf_op jit(solution)/shard_map/all_gather | solution.py:99
  25.9 6.6 %all_gather.35 = bf16[192,768]{0,1:T(8,128)(2,1)S(1)} all-gather(bf16[192,192]{0,1:T(8,128)(2,1)S(1)} %copy.50), channel_id=1, replica_groups=mesh['dp'=4,'ctx'=2,'tensor'=4] {'dp'}, dimensions={1}, use_global_device_ids=true | all-gather | bytes 368640 | tf_op jit(solution)/shard_map/all_gather | solution.py:100
  32.5 7.8 %all_gather.33 = bf16[1024,3,64]{0,2,1:T(8,128)(2,1)S(1)} all-gather(bf16[512,3,64]{0,2,1:T(8,128)(2,1)S(1)} %bitcast.194), channel_id=1, replica_groups=mesh['dp'=4,'ctx'=2,'tensor'=4] {'ctx'}, dimensions={0}, use_global_device_ids=true | all-gather | bytes 589824 | tf_op jit(solution)/shard_map/all_gather | solution.py:122
  40.4 7.0 %all_gather.34 = bf16[1024,3,64]{0,2,1:T(8,128)(2,1)S(1)} all-gather(bf16[512,3,64]{0,2,1:T(8,128)(2,1)S(1)} %add_convert_fusion.1), channel_id=1, replica_groups=mesh['dp'=4,'ctx'=2,'tensor'=4] {'ctx'}, dimensions={0}, use_global_device_ids=true | all-gather | bytes 589824 | tf_op jit(solution)/shard_map/all_gather | solution.py:123
  47.5 9.2 %while.30 = (s32[]{:T(128)}, f32[3,512]{1,0:T(4,128)S(1)}, f32[3,512]{1,0:T(4,128)S(1)}, f32[512,3,64]{0,2,1:T(8,128)S(1)}, s32[2]{0:T(128)S(1)}, /*index=5*/s32...) while((s32[]{:T(128)}, f32[3,512]{1,0:T(4,128)S(1)}, ...), condition=%wide.region_3.4_spmd.clone, body=%wide.region_0.3_spmd.clone.sunk | while | flops 211855360 | bytes 10918577 | solution.py:76
  59.6 68.7 %all-reduce.6.cloned.1.call-done = f32[512,768]{1,0:T(8,128)} async-done(((f32[512,768]{1,0:T(8,128)}), f32[512,768]{1,0:T(8,128)}) %all-reduce.6.cloned.1.call-update) | async-done | bytes 1572880 | tf_op jit(solution)/shard_map/psum | solution.py:133
  131.0 3.7 multiply_convert_fusion.1
  138.2 68.2 %all-reduce.8.cloned.1.call-done = f32[512,768]{1,0:T(8,128)} async-done(((f32[512,768]{1,0:T(8,128)}), f32[512,768]{1,0:T(8,128)}) %all-reduce.8.cloned.1.call-update) | async-done | bytes 1572880 | tf_op jit(solution)/shard_map/psum | solution.py:139
  218.5 67.4 %all-reduce.10.cloned.1.call-done = f32[512,768]{1,0:T(8,128)} async-done(((f32[512,768]{1,0:T(8,128)}), f32[512,768]{1,0:T(8,128)}) %all-reduce.10.cloned.1.call-update) | async-done | bytes 1572880 | tf_op jit(solution)/shard_map/psum | solution.py:155
  293.2 48.6 %while.31 = (s32[]{:T(128)}, f32[512,3,64]{0,2,1:T(8,128)S(1)}, f32[2,512,3,64]{1,0,3,2:T(2,128)}, f32[2,512,3,64]{1,0,3,2:T(2,128)}, bf16[2,512,3,64]{1,3,2,0:T...) while((s32[]{:T(128)}, f32[512,3,64]{0,2,1:T(8,128)S(1)}, ...), condition=%wide.region_17.18_spmd.clone, body=%wide.region_16.17_spmd.clone.sunk | while | flops 513147904 | bytes 22656808 | solution.py:209
  301.4 8.0 %dynamic_update_slice.11 = f32[2,512,3,64]{1,0,3,2:T(2,128)} dynamic-update-slice(f32[2,512,3,64]{1,0,3,2:T(2,128)} %get-tuple-element.565, f32[1,512,3,64]{1,0,3,2:T(1,128)S(1)} %copy.99, s32[]{:T(128)S(6)} %copy.122, s32[]{:T(128)} %constant.61.clone.1..sunk.1, s32[]{:T(128)} %constant.61.clone.1..sunk.1, s32[]{:T(128)} %constant.61.clone.1..sunk.1) | dynamic-update-slice | bytes 786436 | tf_op jit(solution)/shard_map/while/body/jit(dynamic_update_index_in_dim)/dynamic_update_slice | solution.py:209
  309.4 8.0 %dynamic_update_slice.12 = f32[2,512,3,64]{1,0,3,2:T(2,128)} dynamic-update-slice(f32[2,512,3,64]{1,0,3,2:T(2,128)} %get-tuple-element.566, f32[1,512,3,64]{1,0,3,2:T(1,128)S(1)} %copy.100, s32[]{:T(128)S(6)} %copy.122, s32[]{:T(128)} %constant.61.clone.1..sunk.1, s32[]{:T(128)} %constant.61.clone.1..sunk.1, s32[]{:T(128)} %constant.61.clone.1..sunk.1) | dynamic-update-slice | bytes 786436 | tf_op jit(solution)/shard_map/while/body/jit(dynamic_update_index_in_dim)/dynamic_update_slice | solution.py:209
  325.7 8.0 %dynamic_update_slice.11 = f32[2,512,3,64]{1,0,3,2:T(2,128)} dynamic-update-slice(f32[2,512,3,64]{1,0,3,2:T(2,128)} %get-tuple-element.565, f32[1,512,3,64]{1,0,3,2:T(1,128)S(1)} %copy.99, s32[]{:T(128)S(6)} %copy.122, s32[]{:T(128)} %constant.61.clone.1..sunk.1, s32[]{:T(128)} %constant.61.clone.1..sunk.1, s32[]{:T(128)} %constant.61.clone.1..sunk.1) | dynamic-update-slice | bytes 786436 | tf_op jit(solution)/shard_map/while/body/jit(dynamic_update_index_in_dim)/dynamic_update_slice | solution.py:209
  333.7 8.0 %dynamic_update_slice.12 = f32[2,512,3,64]{1,0,3,2:T(2,128)} dynamic-update-slice(f32[2,512,3,64]{1,0,3,2:T(2,128)} %get-tuple-element.566, f32[1,512,3,64]{1,0,3,2:T(1,128)S(1)} %copy.100, s32[]{:T(128)S(6)} %copy.122, s32[]{:T(128)} %constant.61.clone.1..sunk.1, s32[]{:T(128)} %constant.61.clone.1..sunk.1, s32[]{:T(128)} %constant.61.clone.1..sunk.1) | dynamic-update-slice | bytes 786436 | tf_op jit(solution)/shard_map/while/body/jit(dynamic_update_index_in_dim)/dynamic_update_slice | solution.py:209
  362.2 18.7 %reduce-scatter.13.cloned.1.call-done = f32[512,3,64]{0,2,1:T(8,128)} async-done(((f32[1024,3,64]{0,2,1:T(8,128)}), f32[512,3,64]{0,2,1:T(8,128)}) %reduce-scatter.13.cloned.1.call-update) | async-done | bytes 393232 | tf_op jit(solution)/shard_map/reduce_scatter | solution.py:216
  394.4 24.5 %reduce-scatter.21.cloned.1.call-done = f32[96,192]{1,0:T(8,128)} async-done(((f32[768,192]{1,0:T(8,128)}), f32[96,192]{1,0:T(8,128)}) %reduce-scatter.21.cloned.1.call-update) | async-done | bytes 73744
  419.0 5.5 all_gather.39
  425.4 26.3 %all-reduce = (f32[192]{0:T(256)}, f32[192]{0:T(256)}, f32[768]{0:T(1024)}, f32[768]{0:T(1024)}, f32[768]{0:T(1024)}, /*index=5*/f32[768]{0:T(1024)}, f32[768]{0:T(1024)}, f32[768]{0:T(1024)}, f32[768]{0:T(1024)}) all-reduce(f32[192]{0:T(256)S(1)} %reduce_sum.185, ...), channel_id=1, replica_groups=mesh['dp'=4,'ctx'=2,'tensor'=4] {'dp','ctx'}, use_global_device_ids=true, to_apply=%region_23.24 | all-reduce | flops 5760 | bytes 46080 | tf_op jit(solution)/shard_map/psum | solution.py:246
  451.6 13.2 %reduce-scatter.15.cloned.1.call-done = f32[96,768]{1,0:T(8,128)} async-done(((f32[768,768]{1,0:T(8,128)}), f32[96,768]{1,0:T(8,128)}) %reduce-scatter.15.cloned.1.call-update) | async-done | bytes 294928 | tf_op jit(solution)/shard_map/reduce_scatter | solution.py:237
  464.9 9.4 %all_gather.40 = f32[192,768]{1,0:T(8,128)S(1)} all-gather(f32[96,768]{1,0:T(8,128)} %reduce-scatter.15.cloned.1.call-done), channel_id=1, replica_groups=mesh['dp'=4,'ctx'=2,'tensor'=4] {'ctx'}, dimensions={0}, use_global_device_ids=true | all-gather | bytes 884736 | tf_op jit(solution)/shard_map/all_gather | solution.py:243
  474.2 36.1 %reduce-scatter.17.cloned.1.call-done = f32[768,96]{0,1:T(8,128)} async-done(((f32[768,768]{0,1:T(8,128)}), f32[768,96]{0,1:T(8,128)}) %reduce-scatter.17.cloned.1.call-update) | async-done | bytes 294928 | tf_op jit(solution)/shard_map/reduce_scatter | solution.py:238
  510.3 9.4 %all_gather.41 = f32[768,192]{0,1:T(8,128)S(1)} all-gather(f32[768,96]{0,1:T(8,128)} %reduce-scatter.17.cloned.1.call-done), channel_id=1, replica_groups=mesh['dp'=4,'ctx'=2,'tensor'=4] {'ctx'}, dimensions={1}, use_global_device_ids=true | all-gather | bytes 884736 | tf_op jit(solution)/shard_map/all_gather | solution.py:244
  522.5 31.1 %reduce-scatter.19.cloned.1.call-done = f32[96,576]{1,0:T(8,128)} async-done(((f32[768,576]{1,0:T(8,128)}), f32[96,576]{1,0:T(8,128)}) %reduce-scatter.19.cloned.1.call-update) | async-done | bytes 221200
  554.8 11.3 %all_gather.38 = f32[3,192,192]{2,0,1:T(4,128)S(1)} all-gather(f32[3,96,192]{2,0,1:T(4,128)S(1)} %bitcast.191), channel_id=1, replica_groups=mesh['dp'=4,'ctx'=2,'tensor'=4] {'ctx'}, dimensions={1}, use_global_device_ids=true | all-gather | bytes 663552 | tf_op jit(solution)/shard_map/all_gather | solution.py:241
  (217 shorter events, 96.0 us)
Async XLA Ops:
  8.0 120.3 %all-reduce.6.cloned.1.call-start = ((), (), s32[]{:S(2)}) async-start(), calls=%async_computation.6 | async-start | bytes 3145728 | tf_op jit(solution)/shard_map/psum | solution.py:133
  58.4 70.0 %copy-start.31 = (f32[768]{0:T(1024)S(1)}, f32[768]{0:T(1024)}, u32[]{:S(2)}) copy-start(f32[768]{0:T(1024)} %param.27) | copy-start | bytes 9220
  58.4 72.2 %all-gather.3.cloned.1.call-start = ((), (), s32[]{:S(2)}) async-start(), calls=%async_computation.7 | async-start | bytes 1474560 | tf_op jit(solution)/shard_map/all_gather | solution.py:101
  59.0 75.7 %all-gather.5.cloned.1.call-start = ((), (), s32[]{:S(2)}) async-start(), calls=%async_computation.8 | async-start | bytes 1474560 | tf_op jit(solution)/shard_map/all_gather | solution.py:102
  59.6 146.9 %all-reduce.8.cloned.1.call-start = ((), (), s32[]{:S(2)}) async-start(), calls=%async_computation.9 | async-start | bytes 3145728 | tf_op jit(solution)/shard_map/psum | solution.py:139
  130.3 76.2 %copy-start.16 = (f32[512]{0:T(512)}, f32[512]{0:T(512)S(1)}, u32[]{:S(2)}) copy-start(f32[512]{0:T(512)S(1)} %broadcast_multiply_fusion.5) | copy-start | bytes 6148
  130.6 75.8 %copy-start.20 = (f32[512]{0:T(512)}, f32[512]{0:T(512)S(1)}, u32[]{:S(2)}) copy-start(f32[512]{0:T(512)S(1)} %add_rsqrt_fusion.1) | copy-start | bytes 6148
  138.1 68.3 %copy-start.32 = (f32[768]{0:T(1024)S(1)}, f32[768]{0:T(1024)}, u32[]{:S(2)}) copy-start(f32[768]{0:T(1024)} %param.33) | copy-start | bytes 9220
  138.2 147.7 %all-reduce.10.cloned.1.call-start = ((), (), s32[]{:S(2)}) async-start(), calls=%async_computation.10 | async-start | bytes 3145728 | tf_op jit(solution)/shard_map/psum | solution.py:155
  217.6 143.5 %reduce-scatter.11.cloned.1.call-start = ((), (), s32[]{:S(2)}) async-start(), calls=%async_computation.11 | async-start | bytes 1179648 | tf_op jit(solution)/shard_map/reduce_scatter | solution.py:215
  218.5 70.8 %copy-start.17 = (f32[512]{0:T(512)S(1)}, f32[512]{0:T(512)}, u32[]{:S(2)}) copy-start(f32[512]{0:T(512)} %copy-done.16) | copy-start | bytes 6148
  218.5 70.8 %copy-start.19 = (f32[768]{0:T(1024)S(1)}, f32[768]{0:T(1024)}, u32[]{:S(2)}) copy-start(f32[768]{0:T(1024)} %param.28) | copy-start | bytes 9220
  344.4 36.4 %reduce-scatter.13.cloned.1.call-start = ((), (), s32[]{:S(2)}) async-start(), calls=%async_computation.12 | async-start | bytes 1179648 | tf_op jit(solution)/shard_map/reduce_scatter | solution.py:216
  347.3 71.7 %reduce-scatter.21.cloned.1.call-start = ((), (), s32[]{:S(2)}) async-start(), calls=%async_computation.17 | async-start | bytes 884736
  350.1 114.8 %reduce-scatter.15.cloned.1.call-start = ((), (), s32[]{:S(2)}) async-start(), calls=%async_computation.14 | async-start | bytes 2654208 | tf_op jit(solution)/shard_map/reduce_scatter | solution.py:237
  353.8 156.5 %reduce-scatter.17.cloned.1.call-start = ((), (), s32[]{:S(2)}) async-start(), calls=%async_computation.15 | async-start | bytes 2654208 | tf_op jit(solution)/shard_map/reduce_scatter | solution.py:238
  357.6 162.1 %all-reduce.12.cloned.1.call-start = ((), (), s32[]{:S(2)}) async-start(), calls=%async_computation.13 | async-start | bytes 3145728 | tf_op jit(solution)/shard_map/psum | solution.py:232
  384.2 169.4 %reduce-scatter.19.cloned.1.call-start = ((), (), s32[]{:S(2)}) async-start(), calls=%async_computation.16 | async-start | bytes 2211840
  393.0 32.3 %copy-start.23 = (f32[768]{0:T(1024)S(1)}, f32[768]{0:T(1024)}, u32[]{:S(2)}) copy-start(f32[768]{0:T(1024)} %get-tuple-element.292) | copy-start | bytes 9220
  393.0 32.3 %copy-start.24 = (f32[768]{0:T(1024)S(1)}, f32[768]{0:T(1024)}, u32[]{:S(2)}) copy-start(f32[768]{0:T(1024)} %get-tuple-element.352) | copy-start | bytes 9220
  393.1 32.3 %copy-start.26 = (f32[768]{0:T(1024)S(1)}, f32[768]{0:T(1024)}, u32[]{:S(2)}) copy-start(f32[768]{0:T(1024)} %get-tuple-element.350) | copy-start | bytes 9220
  393.1 32.3 %copy-start.27 = (f32[768]{0:T(1024)S(1)}, f32[768]{0:T(1024)}, u32[]{:S(2)}) copy-start(f32[768]{0:T(1024)} %get-tuple-element.290) | copy-start | bytes 9220
  393.1 32.3 %copy-start.28 = (f32[768]{0:T(1024)S(1)}, f32[768]{0:T(1024)}, u32[]{:S(2)}) copy-start(f32[768]{0:T(1024)} %get-tuple-element.295) | copy-start | bytes 9220
  394.2 125.5 %copy-start.1 = (f32[512,768]{1,0:T(8,128)S(1)}, f32[512,768]{1,0:T(8,128)}, u32[]{:S(2)}) copy-start(f32[512,768]{1,0:T(8,128)} %copy-done) | copy-start | bytes 4718596
  (34 other events, 116.1 us)
Sparse Core Ops, SparseCore 0:
  58.5 69.7 all-reduce.5
  138.3 68.1 all-reduce.7
  217.7 68.1 all-reduce.9
  384.4 68.9 all-reduce.11
Sparse Core Ops, SparseCore 1:
  60.4 18.1 all-gather.2
  80.0 17.3 all-gather.4
  344.5 16.6 reduce-scatter.10
  363.4 17.4 reduce-scatter.12
  384.0 34.9 reduce-scatter.20
  422.3 42.5 reduce-scatter.14
  468.1 42.2 reduce-scatter.16
  513.6 40.0 reduce-scatter.18
where the time goes:
time: 579 us; the launch traced here: 576 us
  waiting for transfers between devices  333 us (58%)
  blocking collectives  97.5 us (17%)
  local copies, waits for them, and re-layouts  63.7 us (11%)
  matrix products  38.8 us (7%)
  other arithmetic  23.7 us (4%)
  between operations  15.8 us (3%)
    psum x1, waiting for transfers between devices, per_device(): lax.psum(attn_part, 'tensor')  68.7 us
    psum x1, waiting for transfers between devices, per_device(): second_sum = first_out + lax.psum(down_part, 'tensor') + down_bias  68.2 us
    psum x1, waiting for transfers between devices, per_device(): d_first = lax.psum(first_part, 'tensor') + d_second  67.4 us
    unnamed x14, waiting for transfers between devices  56.9 us
    reduce_scatter x1, waiting for transfers between devices, per_device(): lax.psum_scatter(local_grads[3], ('dp', 'ctx'), scatter_dimension=1, tile...  36.1 us
    dynamic_update_slice x8, local copies, waits for them, and re-layouts, per_device(): lax.scan(back_block, jnp.zeros((row_count, heads_here, HD), jnp.float32),...  33.7 us
    psum x1, blocking collectives, per_device(): lax.psum((grad_query_bias, grad_value_bias, grad_proj_bias, grad_first_ga...  26.3 us
    unnamed x89, local copies, waits for them, and re-layouts  19.3 us
  transfers between devices with their start and end apart: 12, of which 9 were waited for; matrix products, arithmetic and copies ran while one was open for 6% of the time, Pallas kernels for 0%

commit v1 on v0

v1 whole, which is shorter than its diff:
```python
import functools
import math

import jax
import jax.numpy as jnp
from jax import lax
from jax.experimental import pallas as pl
from jax.experimental.pallas import tpu as pltpu
from jax.sharding import PartitionSpec as P

HD = 64


EPSILON = 1e-05
NEGATIVE = -1e30
ROOT_HALF = 0.7071067811865476
ROOT_TWO_PI = 2.5066282746310002
MESH = pl.DeviceIdType.MESH
BF16 = jnp.bfloat16
F32 = jnp.float32
VMEM_SPEC = pl.BlockSpec(memory_space=pltpu.VMEM)
DMA = pltpu.SemaphoreType.DMA


def layer_norm(hidden_in, norm_gain, norm_shift):
    centred = hidden_in - jnp.mean(hidden_in, axis=-1, keepdims=True)
    inverse = lax.rsqrt(jnp.mean(centred * centred, axis=-1, keepdims=True) + EPSILON)
    normed = centred * inverse
    return (normed * norm_gain + norm_shift, normed, inverse)


def norm_back(upstream, normed, inverse, norm_gain):
    scaled = upstream * norm_gain
    return inverse * (
        scaled
        - jnp.mean(scaled, axis=-1, keepdims=True)
        - normed * jnp.mean(scaled * normed, axis=-1, keepdims=True)
    )


def gelu_value(pre_act):
    return 0.5 * pre_act * (1.0 + jax.scipy.special.erf(pre_act * ROOT_HALF))


def gelu_slope(pre_act):
    return (
        0.5 * (1.0 + jax.scipy.special.erf(pre_act * ROOT_HALF))
        + pre_act * jnp.exp(-0.5 * pre_act * pre_act) / ROOT_TWO_PI
    )


def peers_of(axis, size):
    me = lax.axis_index(axis)
    found = []
    for step in range(1, size):
        other = lax.rem(me + step, size)
        found.append((other, {axis: other}))
    return found


def grid_peers(sizes):
    count = sizes["dp"] * sizes["ctx"]
    me = lax.axis_index("dp") * sizes["ctx"] + lax.axis_index("ctx")
    found = []
    for step in range(1, count):
        other = lax.rem(me + step, count)
        found.append((other, {"dp": lax.div(other, sizes["ctx"]), "ctx": lax.rem(other, sizes["ctx"])}))
    return me, found


def greet(groups):
    barrier = pltpu.get_barrier_semaphore()
    total = 0
    for group in groups:
        for _, where in group:
            pl.semaphore_signal(barrier, inc=1, device_id=where, device_id_type=MESH)
            total += 1
    pl.semaphore_wait(barrier, total)


def send_all(pairs, peers, send_sem, recv_sem):
    copies = []
    for step, (other, where) in enumerate(peers):
        source, target = pairs(other)
        copies.append(
            pltpu.make_async_remote_copy(
                src_ref=source,
                dst_ref=target,
                send_sem=send_sem.at[step],
                recv_sem=recv_sem.at[step],
                device_id=where,
                device_id_type=MESH,
            )
        )
        copies[-1].start()
    return copies


def wait_all(copies):
    for copy in copies:
        copy.wait()


def slot_sum(slots, count):
    total = slots[0].astype(F32)
    for index in range(1, count):
        total = total + slots[index].astype(F32)
    return total


def sems(count):
    return [DMA((count,)), DMA((count,))]


def call(kernel, outs, scratch, collective_id, args, name, spec=None):
    return pl.pallas_call(
        kernel,
        out_shape=outs,
        in_specs=[VMEM_SPEC] * len(args),
        out_specs=[VMEM_SPEC] * len(outs),
        scratch_shapes=scratch,
        compiler_params=pltpu.CompilerParams(
            collective_id=collective_id, has_side_effects=True, vmem_limit_bytes=56 * 2**20
        ),
        name=name,
    )(*args)


def shaped(shape, dtype):
    return jax.ShapeDtypeStruct(shape, dtype)


def gather_kernel(sizes, qkv_ref, proj_ref, wide_qkv, wide_proj, *sem):
    me = lax.axis_index("dp")
    peers = peers_of("dp", sizes["dp"])
    greet([peers])
    first = send_all(lambda other: (qkv_ref, wide_qkv.at[:, me]), peers, sem[0], sem[1])
    second = send_all(lambda other: (proj_ref, wide_proj.at[me]), peers, sem[2], sem[3])
    wide_qkv[:, me] = qkv_ref[...]
    wide_proj[me] = proj_ref[...]
    wait_all(first)
    wait_all(second)


def ctx_gather_kernel(sizes, own_ref, wide, *sem):
    me = lax.axis_index("ctx")
    peers = peers_of("ctx", sizes["ctx"])
    greet([peers])
    copies = send_all(lambda other: (own_ref, wide.at[me]), peers, sem[0], sem[1])
    wide[me] = own_ref[...]
    wait_all(copies)


def ctx_sum_kernel(sizes, part_ref, total_ref, slots, *sem):
    me = lax.axis_index("ctx")
    peers = peers_of("ctx", sizes["ctx"])
    greet([peers])
    copies = send_all(lambda other: (part_ref.at[other], slots.at[me]), peers, sem[0], sem[1])
    slots[me] = part_ref[me]
    wait_all(copies)
    total_ref[...] = slot_sum(slots, sizes["ctx"])


def scatter_start(sizes, part_ref, slots, sem):
    me = lax.axis_index("tensor")
    peers = peers_of("tensor", sizes["tensor"])
    copies = send_all(lambda other: (part_ref.at[other], slots.at[me]), peers, sem[0], sem[1])
    slots[me] = part_ref[me]
    return copies


def spread_start(sizes, full_ref, value, sem):
    me = lax.axis_index("tensor")
    peers = peers_of("tensor", sizes["tensor"])
    full_ref[me] = value
    return send_all(lambda other: (full_ref.at[me], full_ref.at[me]), peers, sem[0], sem[1])


def first_kernel(
    sizes, part, tokens, bias, gain, shift, up, down,
    full, out_ref, normed_ref, inverse_ref, wide_up, wide_down,
    slots, *sem
):
    me = lax.axis_index("tensor")
    mine = lax.axis_index("dp")
    others = peers_of("dp", sizes["dp"])
    greet([peers_of("tensor", sizes["tensor"]), others])
    scatter = scatter_start(sizes, part, slots, sem[0:2])
    ups = send_all(lambda other: (up, wide_up.at[mine]), others, sem[4], sem[5])
    downs = send_all(lambda other: (down, wide_down.at[mine]), others, sem[6], sem[7])
    wide_up[mine] = up[...]
    wide_down[mine] = down[...]
    wait_all(scatter)
    first_sum = tokens[me].astype(F32) + slot_sum(slots, sizes["tensor"]) + bias[...]
    first_out, normed, inverse = layer_norm(first_sum, gain[...], shift[...])
    spread = spread_start(sizes, full, first_out.astype(BF16), sem[2:4])
    out_ref[...] = first_out
    normed_ref[...] = normed
    inverse_ref[...] = inverse
    wait_all(ups)
    wait_all(downs)
    wait_all(spread)


def second_kernel(
    sizes, part, first_out, cotangent, bias, gain, shift,
    full, output_ref, back_ref, vector_ref,
    slots, *sem
):
    me = lax.axis_index("tensor")
    greet([peers_of("tensor", sizes["tensor"])])
    scatter = scatter_start(sizes, part, slots, sem[0:2])
    wait_all(scatter)
    second_sum = first_out[...] + slot_sum(slots, sizes["tensor"]) + bias[...]
    result, normed, inverse = layer_norm(second_sum, gain[...], shift[...])
    upstream = cotangent[me].astype(F32)
    d_second = norm_back(upstream, normed, inverse, gain[...])
    spread = spread_start(sizes, full, d_second.astype(BF16), sem[2:4])
    output_ref[...] = result.astype(BF16)
    back_ref[...] = d_second
    vector_ref[0:1] = jnp.sum(upstream, axis=0, keepdims=True)
    vector_ref[1:2] = jnp.sum(upstream * normed, axis=0, keepdims=True)
    vector_ref[2:3] = jnp.sum(d_second, axis=0, keepdims=True)
    wait_all(spread)


def grads_start(sizes, grads, slots, sem):
    mine = lax.axis_index("dp")
    others = peers_of("dp", sizes["dp"])
    copies = send_all(lambda other: (grads.at[other], slots.at[mine]), others, sem[0], sem[1])
    slots[mine] = grads[mine]
    return copies


def grads_middle(sizes, copies, slots, blocks, sem):
    wait_all(copies)
    me = lax.axis_index("ctx")
    blocks[me] = slot_sum(slots, sizes["dp"]).astype(BF16)
    return send_all(
        lambda other: (blocks.at[me], blocks.at[me]), peers_of("ctx", sizes["ctx"]), sem[0], sem[1]
    )


def third_kernel(
    sizes, part, d_second, normed_ref, inverse_ref, gain, grads_a, grads_b,
    full, back_ref, vector_ref, owned_a, owned_b,
    slots, slots_a, slots_b, blocks_a, blocks_b, *sem
):
    greet(
        [
            peers_of("tensor", sizes["tensor"]),
            peers_of("dp", sizes["dp"]),
            peers_of("ctx", sizes["ctx"]),
        ]
    )
    scatter = scatter_start(sizes, part, slots, sem[0:2])
    moving_a = grads_start(sizes, grads_a, slots_a, sem[4:6])
    moving_b = grads_start(sizes, grads_b, slots_b, sem[6:8])
    wait_all(scatter)
    d_first = slot_sum(slots, sizes["tensor"]) + d_second[...]
    normed = normed_ref[...]
    d_attn = norm_back(d_first, normed, inverse_ref[...], gain[...])
    spread = spread_start(sizes, full, d_attn.astype(BF16), sem[2:4])
    back_ref[...] = d_attn
    vector_ref[0:1] = jnp.sum(d_first, axis=0, keepdims=True)
    vector_ref[1:2] = jnp.sum(d_first * normed, axis=0, keepdims=True)
    vector_ref[2:3] = jnp.sum(d_attn, axis=0, keepdims=True)
    moving_a = grads_middle(sizes, moving_a, slots_a, blocks_a, sem[8:10])
    moving_b = grads_middle(sizes, moving_b, slots_b, blocks_b, sem[10:12])
    wait_all(moving_a)
    owned_a[...] = slot_sum(blocks_a, sizes["ctx"])
    wait_all(moving_b)
    owned_b[...] = slot_sum(blocks_b, sizes["ctx"])
    wait_all(spread)


def last_kernel(
    sizes, part, d_attn, grads, vectors,
    full, owned, vector_ref,
    slots, slots_g, blocks, slots_v, grid_v, *sem
):
    me = lax.axis_index("tensor")
    rows = peers_of("tensor", sizes["tensor"])
    here, everyone = grid_peers(sizes)
    greet([rows, everyone])
    small = send_all(lambda other: (vectors, slots_v.at[me]), rows, sem[8], sem[9])
    slots_v[me] = vectors[...]
    scatter = scatter_start(sizes, part, slots, sem[0:2])
    moving = grads_start(sizes, grads, slots_g, sem[4:6])
    wait_all(small)
    own = vectors[...]
    row_ids = lax.broadcasted_iota(jnp.int32, own.shape, 0)
    grid_v[here] = jnp.where(row_ids < 6, slot_sum(slots_v, sizes["tensor"]), own)
    small = send_all(lambda other: (grid_v.at[here], grid_v.at[here]), everyone, sem[10], sem[11])
    wait_all(scatter)
    d_tokens = slot_sum(slots, sizes["tensor"]) + d_attn[...]
    spread = spread_start(sizes, full, d_tokens.astype(BF16), sem[2:4])
    moving = grads_middle(sizes, moving, slots_g, blocks, sem[6:8])
    wait_all(small)
    vector_ref[...] = slot_sum(grid_v, sizes["dp"] * sizes["ctx"])
    wait_all(moving)
    owned[...] = slot_sum(blocks, sizes["ctx"])
    wait_all(spread)


CONTRACT_LAST = (((1,), (1,)), ((), ()))
CONTRACT_FIRST = (((0,), (0,)), ((), ()))


def forward_kernel(score_scale, length_ref, q_ref, k_ref, v_ref, out_ref, low_ref, log_ref):
    length = length_ref[0]
    rows, width = q_ref.shape
    keys = k_ref.shape[0]
    block = math.gcd(rows, 256)
    valid = lax.broadcasted_iota(jnp.int32, (block, keys), 1) < length

    @pl.loop(0, rows // block)
    def _(step):
        here = pl.ds(pl.multiple_of(step * block, block), block)
        for head in range(width // HD):
            lanes = slice(head * HD, (head + 1) * HD)
            scores = lax.dot_general(
                q_ref[here, lanes], k_ref[:, lanes], CONTRACT_LAST, preferred_element_type=F32
            ) * score_scale
            scores = jnp.where(valid, scores, NEGATIVE)
            top = jnp.max(scores, axis=-1, keepdims=True)
            weights = jnp.where(valid, jnp.exp(scores - top), 0.0)
            total = jnp.sum(weights, axis=-1, keepdims=True)
            acc = jnp.dot(weights.astype(BF16), v_ref[:, lanes], preferred_element_type=F32)
            attended = acc / total
            out_ref[here, lanes] = attended
            low_ref[here, lanes] = attended.astype(BF16)
            log_ref[here, head : head + 1] = top + jnp.log(total)


def backward_kernel(
    score_scale, length_ref, q_ref, k_ref, v_ref, heads_ref, attended_ref, log_ref,
    dq_ref, dk_ref, dv_ref
):
    length = length_ref[0]
    rows, width = q_ref.shape
    keys = k_ref.shape[0]
    block = math.gcd(rows, 256)
    valid = lax.broadcasted_iota(jnp.int32, (block, keys), 1) < length
    dk_ref[...] = jnp.zeros_like(dk_ref)
    dv_ref[...] = jnp.zeros_like(dv_ref)

    @pl.loop(0, rows // block)
    def _(step):
        here = pl.ds(pl.multiple_of(step * block, block), block)
        for head in range(width // HD):
            lanes = slice(head * HD, (head + 1) * HD)
            q, k, v, d_heads = q_ref[here, lanes], k_ref[:, lanes], v_ref[:, lanes], heads_ref[here, lanes]
            delta = jnp.sum(d_heads.astype(F32) * attended_ref[here, lanes], axis=-1, keepdims=True)
            scores = lax.dot_general(q, k, CONTRACT_LAST, preferred_element_type=F32) * score_scale
            scores = jnp.where(valid, scores, NEGATIVE)
            probs = jnp.where(valid, jnp.exp(scores - log_ref[here, head : head + 1]), 0.0)
            d_probs = lax.dot_general(d_heads, v, CONTRACT_LAST, preferred_element_type=F32)
            d_scores = (probs * (d_probs - delta)).astype(BF16)
            dv_ref[:, lanes] += lax.dot_general(
                probs.astype(BF16), d_heads, CONTRACT_FIRST, preferred_element_type=F32
            )
            dk_ref[:, lanes] += lax.dot_general(
                d_scores, q, CONTRACT_FIRST, preferred_element_type=F32
            ) * score_scale
            dq_ref[here, lanes] = jnp.dot(d_scores, k, preferred_element_type=F32) * score_scale


def attention_call(kernel, outs, args, name):
    return pl.pallas_call(
        kernel,
        out_shape=outs,
        in_specs=[pl.BlockSpec(memory_space=pltpu.SMEM)] + [VMEM_SPEC] * (len(args) - 1),
        out_specs=[VMEM_SPEC] * len(outs),
        compiler_params=pltpu.CompilerParams(vmem_limit_bytes=56 * 2**20),
        name=name,
    )(*args)


def per_device(
    sizes,
    tokens,
    lengths,
    cotangent,
    qkv_weight,
    query_bias,
    value_bias,
    proj_weight,
    proj_bias,
    first_gain,
    first_shift,
    up_weight,
    up_bias,
    down_weight,
    down_bias,
    second_gain,
    second_shift,
):
    data, blocks, ranks = sizes["dp"], sizes["ctx"], sizes["tensor"]
    rows_in = tokens[0]
    row_count, model = rows_in.shape
    part_rows = row_count // ranks
    piece, local_width = qkv_weight.shape[1:]
    up_width = up_weight.shape[1]
    score_scale = 1.0 / math.sqrt(HD)
    split = (ranks, part_rows, model)
    part_slots = pltpu.VMEM(split, BF16)
    local = shaped((part_rows, model), F32)
    row = lambda vector: vector[None]

    wide_qkv, wide_proj = call(
        functools.partial(gather_kernel, sizes),
        [shaped((3, data, piece, local_width), BF16), shaped((data,) + proj_weight.shape, BF16)],
        sems(data - 1) * 2,
        0,
        (qkv_weight, proj_weight),
        "gather_weights",
    )
    wide_qkv = wide_qkv.reshape(3, model, local_width)
    wide_proj = wide_proj.transpose(1, 0, 2).reshape(local_width, model)

    projected = jnp.einsum("td,ide->ite", rows_in, wide_qkv, preferred_element_type=F32)
    queries = (projected[0] + query_bias).astype(BF16)
    own_kv = jnp.concatenate(
        [projected[1].astype(BF16), (projected[2] + value_bias).astype(BF16)], axis=1
    )
    (kv,) = call(
        functools.partial(ctx_gather_kernel, sizes),
        [shaped((blocks,) + own_kv.shape, BF16)],
        sems(blocks - 1),
        1,
        (own_kv,),
        "gather_keys",
    )
    kv = kv.reshape(blocks * row_count, 2 * local_width)
    keys, values = kv[:, :local_width], kv[:, local_width:]
    attended, attended_low, log_total = attention_call(
        functools.partial(forward_kernel, score_scale),
        [
            shaped((row_count, local_width), F32),
            shaped((row_count, local_width), BF16),
            shaped((row_count, local_width // HD), F32),
        ],
        (lengths, queries, keys, values),
        "attention_forward",
    )
    attn_part = jnp.dot(attended_low, wide_proj, preferred_element_type=F32).astype(BF16)

    first_low, first_out, first_normed, first_inverse, wide_up, wide_down = call(
        functools.partial(first_kernel, sizes),
        [
            shaped(split, BF16),
            local,
            local,
            shaped((part_rows, 1), F32),
            shaped((data,) + up_weight.shape, BF16),
            shaped((data,) + down_weight.shape, BF16),
        ],
        [part_slots] + sems(ranks - 1) * 2 + sems(data - 1) * 2,
        2,
        (
            attn_part.reshape(split),
            rows_in.reshape(split),
            row(proj_bias),
            row(first_gain),
            row(first_shift),
            up_weight,
            down_weight,
        ),
        "first_norm",
    )
    first_low = first_low.reshape(row_count, model)
    wide_up = wide_up.reshape(model, up_width)
    wide_down = wide_down.transpose(1, 0, 2).reshape(up_width, model)

    pre_act = jnp.dot(first_low, wide_up, preferred_element_type=F32) + up_bias
    hidden = gelu_value(pre_act).astype(BF16)
    down_part = jnp.dot(hidden, wide_down, preferred_element_type=F32).astype(BF16)
    d_second_low, output_part, d_second, second_vectors = call(
        functools.partial(second_kernel, sizes),
        [shaped(split, BF16), shaped((part_rows, model), BF16), local, shaped((3, model), F32)],
        [part_slots] + sems(ranks - 1) * 2,
        3,
        (
            down_part.reshape(split),
            first_out,
            cotangent[0].reshape(split),
            row(down_bias),
            row(second_gain),
            row(second_shift),
        ),
        "second_norm",
    )
    output = lax.all_gather(output_part, "tensor", axis=0, tiled=True)[None]
    d_second_low = d_second_low.reshape(row_count, model)
    grad_down = jnp.einsum("td,tf->df", d_second_low, hidden, preferred_element_type=F32)
    d_hidden = jnp.einsum("td,fd->tf", d_second_low, wide_down, preferred_element_type=F32)
    d_pre = d_hidden * gelu_slope(pre_act)
    grad_up_bias = jnp.sum(d_pre, axis=0)
    d_pre_low = d_pre.astype(BF16)
    grad_up = jnp.einsum("td,tf->df", first_low, d_pre_low, preferred_element_type=F32)
    first_part = jnp.einsum("tf,df->td", d_pre_low, wide_up, preferred_element_type=F32).astype(BF16)

    grad_shape = (data, model // data, up_width)
    grad_slots = pltpu.VMEM(grad_shape, BF16)
    ctx_slots = pltpu.VMEM((blocks,) + grad_shape[1:], BF16)
    d_attn_low, d_attn, first_vectors, own_up, own_down = call(
        functools.partial(third_kernel, sizes),
        [shaped(split, BF16), local, shaped((3, model), F32)] + [shaped(grad_shape[1:], F32)] * 2,
        [part_slots, grad_slots, grad_slots, ctx_slots, ctx_slots]
        + sems(ranks - 1) * 2
        + sems(data - 1) * 2
        + sems(blocks - 1) * 2,
        4,
        (
            first_part.reshape(split),
            d_second,
            first_normed,
            first_inverse,
            row(first_gain),
            grad_up.astype(BF16).reshape(grad_shape),
            grad_down.astype(BF16).reshape(grad_shape),
        ),
        "first_norm_back",
    )
    d_attn_low = d_attn_low.reshape(row_count, model)
    d_heads = jnp.einsum("td,ed->te", d_attn_low, wide_proj, preferred_element_type=F32).astype(BF16)
    d_query, key_grads, value_grads = attention_call(
        functools.partial(backward_kernel, score_scale),
        [shaped((row_count, local_width), F32)]
        + [shaped((blocks * row_count, local_width), F32)] * 2,
        (lengths, queries, keys, values, d_heads, attended, log_total),
        "attention_backward",
    )
    kv_part = jnp.concatenate([key_grads.astype(BF16), value_grads.astype(BF16)], axis=1)
    kv_shape = (blocks, row_count, 2 * local_width)
    (own_grads,) = call(
        functools.partial(ctx_sum_kernel, sizes),
        [shaped(kv_shape[1:], F32)],
        [pltpu.VMEM(kv_shape, BF16)] + sems(blocks - 1),
        5,
        (kv_part.reshape(kv_shape),),
        "sum_keys",
    )
    grad_query_bias = jnp.sum(d_query, axis=0)
    grad_value_bias = jnp.sum(own_grads[:, local_width:], axis=0)
    d_stack = jnp.concatenate([d_query.astype(BF16), own_grads.astype(BF16)], axis=1)
    grad_qkv = jnp.einsum("td,te->de", rows_in, d_stack, preferred_element_type=F32)
    grad_proj = jnp.einsum("td,te->de", d_attn_low, attended_low, preferred_element_type=F32)
    flat_qkv = wide_qkv.transpose(1, 0, 2).reshape(model, 3 * local_width)
    input_part = jnp.einsum("te,de->td", d_stack, flat_qkv, preferred_element_type=F32).astype(BF16)

    last_shape = (data, model // data, 4 * local_width)
    last_grads = jnp.concatenate([grad_qkv.astype(BF16), grad_proj.astype(BF16)], axis=1)
    vector_width = max(model, up_width, 2 * local_width)
    pad = lambda array: jnp.pad(array, ((0, 0), (0, vector_width - array.shape[1])))
    vectors = jnp.concatenate(
        [
            pad(second_vectors),
            pad(first_vectors),
            pad(grad_up_bias[None]),
            pad(jnp.concatenate([grad_query_bias, grad_value_bias])[None]),
        ]
    )
    grad_tokens, own_last, sums = call(
        functools.partial(last_kernel, sizes),
        [shaped(split, BF16), shaped(last_shape[1:], F32), shaped(vectors.shape, F32)],
        [
            part_slots,
            pltpu.VMEM(last_shape, BF16),
            pltpu.VMEM((blocks,) + last_shape[1:], BF16),
            pltpu.VMEM((ranks,) + vectors.shape, F32),
            pltpu.VMEM((data * blocks,) + vectors.shape, F32),
        ]
        + sems(ranks - 1) * 2
        + sems(data - 1)
        + sems(blocks - 1)
        + sems(ranks - 1)
        + sems(data * blocks - 1),
        6,
        (input_part.reshape(split), d_attn, last_grads.reshape(last_shape), vectors),
        "token_grads",
    )
    grad_tokens = grad_tokens.reshape(1, row_count, model).astype(F32)
    own_qkv = own_last[:, : 3 * local_width].reshape(-1, 3, local_width).transpose(1, 0, 2)
    return (
        output,
        grad_tokens,
        own_qkv,
        sums[7, :local_width],
        sums[7, local_width : 2 * local_width],
        own_last[:, 3 * local_width :].T,
        sums[5, :model],
        sums[4, :model],
        sums[3, :model],
        own_up,
        sums[6, :up_width],
        own_down.T,
        sums[2, :model],
        sums[1, :model],
        sums[0, :model],
    )


def solution(mesh):
    placed = (
        P("dp", "ctx", None),
        P("dp"),
        P("dp", "ctx", None),
        P(None, "dp", "tensor"),
        P("tensor"),
        P("tensor"),
        P("tensor", "dp"),
        P(),
        P(),
        P(),
        P("dp", "tensor"),
        P("tensor"),
        P("tensor", "dp"),
        P(),
        P(),
        P(),
    )
    return jax.shard_map(
        functools.partial(per_device, dict(mesh.shape)),
        mesh=mesh,
        in_specs=placed,
        out_specs=(
            P("dp", "ctx", None),
            P("dp", "ctx", None),
            P(None, "dp", "tensor"),
            P("tensor"),
            P("tensor"),
            P("tensor", "dp"),
            P(),
            P(),
            P(),
            P("dp", "tensor"),
            P("tensor"),
            P("tensor", "dp"),
            P(),
            P(),
            P(),
        ),
        check_vma=False,
    )
```

time: 579 us -> 308 us (0.53)
  waiting for transfers between devices: 333 us -> 0 us
  Pallas kernels: 0 us -> 228 us
  blocking collectives: 97.5 us -> 20.4 us
  local copies, waits for them, and re-layouts: 63.7 us -> 28.5 us
  matrix products: 38.8 us -> 19.9 us
  other arithmetic: 23.7 us -> 7.71 us
  between operations: 15.8 us -> 1.64 us
    pallas_call x0 -> x9, Pallas kernels: none -> 228 us  [the longest x7 214 us: call(): pl.pallas_call(kernel, out_shape=outs, in_specs=[VMEM_SPEC] * len(args),...]
    psum x4 -> x0, waiting for transfers between devices: 204 us -> none  [the longest x1 68.7 us: per_device(): lax.psum(attn_part, 'tensor')]
    reduce_scatter x4 -> x0, waiting for transfers between devices: 71.4 us -> none  [the longest x1 36.1 us: per_device(): lax.psum_scatter(local_grads[3], ('dp', 'ctx'), scatter_dimension=1, tile...]
    unnamed x14 -> x0, waiting for transfers between devices: 56.9 us -> none
    all_gather x8 -> x1, blocking collectives: 71.3 us -> 20.4 us  [per_device(): output = lax.all_gather(output_part, 'tensor', axis=0, tiled=True)[None]]
    dynamic_update_slice x8 -> x0, local copies, waits for them, and re-layouts: 33.7 us -> none  [per_device(): lax.scan(back_block, jnp.zeros((row_count, heads_here, HD), jnp.float32),...]
    psum x1 -> x0, blocking collectives: 26.3 us -> none  [per_device(): lax.psum((grad_query_bias, grad_value_bias, grad_proj_bias, grad_first_ga...]
    dot_general x25 -> x12, matrix products: 36.1 us -> 19.9 us  [the longest x1 2.26 us: per_device(): jnp.einsum('td,fd->tf', d_second_low, wide_down, preferred_element_type=F32)]
  transfers between devices with their start and end apart: 12 -> 0, of which waited for: 9 -> 0; matrix products, arithmetic and copies ran while one was open for 6% -> 0% of each run, Pallas kernels for 0% -> 0%
where the time goes in v1:
time: 308 us; the launch traced here: 306 us
  Pallas kernels  228 us (74%)
  local copies, waits for them, and re-layouts  28.5 us (9%)
  blocking collectives  20.4 us (7%)
  matrix products  19.9 us (6%)
  other arithmetic  7.71 us (3%)
    pallas_call x7, Pallas kernels, call(): pl.pallas_call(kernel, out_shape=outs, in_specs=[VMEM_SPEC] * len(args),...  214 us
    all_gather x1, blocking collectives, per_device(): output = lax.all_gather(output_part, 'tensor', axis=0, tiled=True)[None]  20.4 us
    pallas_call x2, Pallas kernels, attention_call(): pl.pallas_call(kernel, out_shape=outs, in_specs=[pl.BlockSpec(memory_spac...  14.4 us
    broadcast_in_dim x6, local copies, waits for them, and re-layouts, per_device(): row = lambda vector: vector[None]  7.6 us
    unnamed x44, local copies, waits for them, and re-layouts  6.57 us

profile of v1, /device:TPU:0, one launch (start us, length us, event | category | flops | bytes accessed | tf_op | source)
XLA Modules:
  0.0 306.3 jit_solution(2364626191186869693)
XLA Ops:
  8.9 1.9 copy.52.down
  10.8 22.6 %gather_weights.1 = (bf16[3,4,192,192]{3,2,1,0:T(8,128)(2,1)}, bf16[4,192,192]{2,1,0:T(8,128)(2,1)}) custom-call(bf16[3,192,192]{2,1,0:T(8,128)(2,1)} %qkv_ref.1, bf16[192,192]{1,0:T(8,128)(2,1)} %proj_ref.1), custom_call_target="tpu_custom_call" | custom-call | tf_op jit(solution)/shard_map/gather_weights/pallas_call | solution.py:116
  38.4 13.6 %gather_keys.1 = bf16[2,512,384]{2,1,0:T(8,128)(2,1)} custom-call(bf16[512,384]{1,0:T(8,128)(2,1)} %pad_maximum_fusion.5.own_ref), custom_call_target="tpu_custom_call" | custom-call | tf_op jit(solution)/shard_map/gather_keys/pallas_call | solution.py:116
  52.0 2.4 fusion.17
  54.4 5.7 %attention_forward.1 = (f32[512,192]{1,0:T(8,128)}, bf16[512,192]{1,0:T(8,128)(2,1)}, f32[512,3]{1,0:T(8,128)}) custom-call(s32[1]{0:T(128)S(6)} %copy.65.length_ref, bf16[512,192]{1,0:T(8,128)(2,1)} %get-tuple-element.120.q_ref, bf16[1024,192]{1,0:T(8,128)(2,1)} %get-tuple-element.122.k_ref, bf16[1024,192]{1,0:T(8,128)(2,1)} %get-tuple-element.121.v_ref), custom_call_target="tpu_custom_call" | custom-call | tf_op jit(solution)/shard_map/attention_forward/pallas_call | solution.py:370
  60.1 2.2 convolution_convert_fusion.6
  62.3 39.7 %first_norm.1 = (bf16[4,128,768]{2,1,0:T(8,128)(2,1)}, f32[128,768]{1,0:T(8,128)}, f32[128,768]{1,0:T(8,128)}, f32[128,1]{1,0:T(8,128)}, bf16[4,192,768]{2,1,0:T(8,128)(2,1)}, /*index=5*/bf16[4,768,192]{2,1,0:T(8,128)(2,1)}) custom-call(bf16[4,128,768]{2,1,0:T(8,128)(2,1)} %bitcast.85, bf16[4,128,768]{2,1,0:T(8,128)(2,1)} %bitcast.97, ...), custom_call_target="tpu_custom_call" | custom-call | tf_op jit(solution)/shard_map/first_norm/pallas_call | solution.py:116
  102.0 1.8 copy.53
  103.8 2.0 multiply_convert_fusion
  105.8 1.7 convolution_convert_fusion.4
  107.5 39.9 %second_norm.1 = (bf16[4,128,768]{2,1,0:T(8,128)(2,1)}, bf16[128,768]{1,0:T(8,128)(2,1)}, f32[128,768]{1,0:T(8,128)}, f32[3,768]{1,0:T(4,128)}) custom-call(bf16[4,128,768]{2,1,0:T(8,128)(2,1)} %bitcast.96, f32[128,768]{1,0:T(8,128)} %get-tuple-element.47.first_out, bf16[4,128,768]{2,1,0:T(8,128)(2,1)} %bitcast.95, f32[1,768]{1,0:T(1,128)} %broadcast_in_dim.34.bias, ...), custom_call_target="tpu_custom_call" | custom-call | tf_op jit(solution)/shard_map/second_norm/pallas_call | solution.py:116
  147.4 2.3 fusion.20
  149.6 1.8 convolution_convert_fusion
  151.5 1.7 convolution_convert_fusion.3
  153.2 1.8 convolution_convert_fusion.1
  155.0 44.7 %first_norm_back.1 = (bf16[4,128,768]{2,1,0:T(8,128)(2,1)}, f32[128,768]{1,0:T(8,128)}, f32[3,768]{1,0:T(4,128)}, f32[192,768]{1,0:T(8,128)}, f32[192,768]{1,0:T(8,128)}) custom-call(bf16[4,128,768]{2,1,0:T(8,128)(2,1)} %bitcast.100, f32[128,768]{1,0:T(8,128)} %get-tuple-element.50.d_second, f32[128,768]{1,0:T(8,128)} %get-tuple-element.51.normed_ref, ...), custom_call_target="tpu_custom_call" | custom-call | tf_op jit(solution)/shard_map/first_norm_back/pallas_call | solution.py:116
  199.7 1.5 convolution_convert_fusion.8
  201.3 1.5 convolution_convert_fusion.7
  203.6 8.8 %attention_backward.1 = (f32[512,192]{1,0:T(8,128)}, f32[1024,192]{1,0:T(8,128)}, f32[1024,192]{1,0:T(8,128)}) custom-call(s32[1]{0:T(128)S(6)} %copy.65.length_ref, bf16[512,192]{1,0:T(8,128)(2,1)} %get-tuple-element.120.q_ref, bf16[1024,192]{1,0:T(8,128)(2,1)} %get-tuple-element.122.k_ref, bf16[1024,192]{1,0:T(8,128)(2,1)} %get-tuple-element.121.v_ref, ...), custom_call_target="tpu_custom_call" | custom-call | tf_op jit(solution)/shard_map/attention_backward/pallas_call | solution.py:370
  215.2 13.7 %sum_keys.1 = f32[512,384]{1,0:T(8,128)} custom-call(bf16[2,512,384]{2,1,0:T(8,128)(2,1)} %bitcast.81), custom_call_target="tpu_custom_call" | custom-call | tf_op jit(solution)/shard_map/sum_keys/pallas_call | solution.py:116
  230.3 1.7 convolution_convert_fusion.5
  235.1 39.7 %token_grads.1 = (bf16[4,128,768]{2,1,0:T(8,128)(2,1)}, f32[192,768]{1,0:T(8,128)}, f32[8,768]{1,0:T(8,128)}) custom-call(bf16[4,128,768]{2,1,0:T(8,128)(2,1)} %bitcast.99, f32[128,768]{1,0:T(8,128)} %get-tuple-element.59.d_attn, bf16[4,192,768]{2,1,0:T(8,128)(2,1)} %bitcast.79, f32[8,768]{1,0:T(8,128)} %select_maximum_fusion.vectors), custom_call_target="tpu_custom_call" | custom-call | tf_op jit(solution)/shard_map/token_grads/pallas_call | solution.py:116
  276.3 1.7 slice_reduce_fusion.1
  282.1 20.4 %all_gather.3 = bf16[512,768]{1,0:T(8,128)(2,1)S(1)} all-gather(bf16[128,768]{1,0:T(8,128)(2,1)S(1)} %copy-done.10), channel_id=1, replica_groups=mesh['dp'=4,'ctx'=2,'tensor'=4] {'tensor'}, dimensions={0}, use_global_device_ids=true | all-gather | bytes 983040 | tf_op jit(solution)/shard_map/all_gather | solution.py:494
  (74 shorter events, 30.1 us)
Async XLA Ops:
  33.4 1.8 copy-start.1
  34.8 1.1 copy-start.4
  35.9 0.8 copy-start.13
  35.9 0.8 copy-start.14
  102.0 1.8 copy-start.15
  102.0 1.8 copy-start.18
  147.4 2.3 copy-start.17
  151.5 1.7 copy-start.16
  155.0 46.2 %copy-start.3 = (bf16[512,192]{1,0:T(8,128)(2,1)S(1)}, bf16[512,192]{1,0:T(8,128)(2,1)}, u32[]{:S(2)}) copy-start(bf16[512,192]{1,0:T(8,128)(2,1)} %get-tuple-element.42) | copy-start | bytes 589828
  212.4 1.5 copy-start.2
  214.0 14.9 %copy-start.9 = (f32[512,192]{1,0:T(8,128)S(1)}, f32[512,192]{1,0:T(8,128)}, u32[]{:S(2)}) copy-start(f32[512,192]{1,0:T(8,128)} %get-tuple-element.56) | copy-start | bytes 1179652
  228.8 1.4 copy-start
  230.3 1.8 copy-start.11
  230.3 1.8 copy-start.12
  230.3 2.4 copy-start.5
  280.0 2.1 copy-start.10
  280.8 21.7 %copy-start.6 = (bf16[4,128,768]{2,1,0:T(8,128)(2,1)S(1)}, bf16[4,128,768]{2,1,0:T(8,128)(2,1)}, u32[]{:S(2)}) copy-start(bf16[4,128,768]{2,1,0:T(8,128)(2,1)} %get-tuple-element.62) | copy-start | bytes 2359300
  302.6 2.1 copy-start.8
  303.8 1.7 copy-start.7

commit v2 on v1

--- a/solution.py
+++ b/solution.py
@@ -130,177 +130,404 @@
     return jax.ShapeDtypeStruct(shape, dtype)
 
 
-def gather_kernel(sizes, qkv_ref, proj_ref, wide_qkv, wide_proj, *sem):
+def pair_roles(size):
     me = lax.axis_index("dp")
-    peers = peers_of("dp", sizes["dp"])
-    greet([peers])
-    first = send_all(lambda other: (qkv_ref, wide_qkv.at[:, me]), peers, sem[0], sem[1])
-    second = send_all(lambda other: (proj_ref, wide_proj.at[me]), peers, sem[2], sem[3])
-    wide_qkv[:, me] = qkv_ref[...]
-    wide_proj[me] = proj_ref[...]
-    wait_all(first)
-    wait_all(second)
-
-
-def ctx_gather_kernel(sizes, own_ref, wide, *sem):
+    partner = me + 1 - 2 * lax.rem(me, 2)
+    far = [(lax.rem(me + 2 * step, size), lax.rem(me + size - 2 * step, size)) for step in range(1, size // 2)]
+    return me, partner, far
+
+
+def pair_group(size):
+    me, partner, far = pair_roles(size)
+    return [(partner, {"dp": partner})] + [(to, {"dp": to}) for to, _ in far]
+
+
+def remote(source, target, send, recv, where):
+    return pltpu.make_async_remote_copy(
+        src_ref=source, dst_ref=target, send_sem=send, recv_sem=recv, device_id=where, device_id_type=MESH
+    )
+
+
+def pair_sems(size):
+    return sems(1) + sems(max(1, size // 2 - 1)) * 2
+
+
+def gather_start(size, own_ref, place, sem):
+    me, partner, far = pair_roles(size)
+    near = remote(own_ref, place(me), sem[0].at[0], sem[1].at[0], {"dp": partner})
+    wide = [
+        remote(own_ref, place(me), sem[2].at[step], sem[3].at[step], {"dp": to})
+        for step, (to, _) in enumerate(far)
+    ]
+    for copy in wide + [near]:
+        copy.start()
+    return near, wide
+
+
+def gather_pass(size, copies, place, sem):
+    me, partner, far = pair_roles(size)
+    passed = []
+    for step, (_, origin) in enumerate(far):
+        copies[1][step].wait()
+        passed.append(
+            remote(place(origin), place(origin), sem[4].at[step], sem[5].at[step], {"dp": partner})
+        )
+        passed[-1].start()
+    return [copies[0]] + passed
+
+
+def gather_kernel(sizes, qkv_ref, wide_qkv, *sem):
+    size = sizes["dp"]
+    greet([pair_group(size)])
+    place = lambda index: wide_qkv.at[:, index]
+    copies = gather_start(size, qkv_ref, place, sem)
+    wide_qkv[:, lax.axis_index("dp")] = qkv_ref[...]
+    wait_all(gather_pass(size, copies, place, sem))
+
+
+def ctx_gather_kernel(sizes, own_ref, proj_ref, wide, wide_proj, *sem):
     me = lax.axis_index("ctx")
+    size = sizes["dp"]
     peers = peers_of("ctx", sizes["ctx"])
-    greet([peers])
+    greet([peers, pair_group(size)])
     copies = send_all(lambda other: (own_ref, wide.at[me]), peers, sem[0], sem[1])
+    place = lambda index: wide_proj.at[index]
+    projs = gather_start(size, proj_ref, place, sem[2:])
     wide[me] = own_ref[...]
+    wide_proj[lax.axis_index("dp")] = proj_ref[...]
+    wait_all(gather_pass(size, projs, place, sem[2:]))
     wait_all(copies)
 
 
-def ctx_sum_kernel(sizes, part_ref, total_ref, slots, *sem):
+LAG = 2
+
+
+def line_roles(size):
+    me = lax.axis_index("tensor")
+    lower, upper = lax.rem(me + size - 1, size), lax.rem(me + 1, size)
+    return [(me, lower, upper), (size - 1 - me, upper, lower)]
+
+
+def greet_line(size, groups):
+    me = lax.axis_index("tensor")
+    barrier = pltpu.get_barrier_semaphore()
+
+    @pl.when(me > 0)
+    def _():
+        pl.semaphore_signal(barrier, inc=1, device_id={"tensor": me - 1}, device_id_type=MESH)
+
+    @pl.when(me < size - 1)
+    def _():
+        pl.semaphore_signal(barrier, inc=1, device_id={"tensor": me + 1}, device_id_type=MESH)
+
+    total = 0
+    for group in groups:
+        for _, where in group:
+            pl.semaphore_signal(barrier, inc=1, device_id=where, device_id_type=MESH)
+            total += 1
+
+    beside = jnp.where(me > 0, 1, 0) + jnp.where(me < size - 1, 1, 0)
+    pl.semaphore_wait(barrier, total + beside)
+
+
+def both(*conditions):
+    return functools.reduce(jnp.logical_and, conditions)
+
+
+def line_start(size, part, slots, sem):
+    count = part.shape[1]
+    for flow, (place, toward, _) in enumerate(line_roles(size)):
+
+        @pl.when(place == size - 1)
+        def _(flow=flow, toward=toward):
+            @pl.loop(0, count)
+            def _(k):
+                remote(
+                    part.at[flow, k], slots.at[flow, k], sem[0].at[flow, k], sem[1].at[flow, k], {"tensor": toward}
+                ).start()
+
+
+def line_run(size, part, slots, sums, full, sem, finish):
+    count = part.shape[1]
+    roles = line_roles(size)
+
+    def reduce_copy(flow, k, source):
+        return remote(
+            source.at[flow, k], slots.at[flow, k], sem[0].at[flow, k], sem[1].at[flow, k], {"tensor": roles[flow][1]}
+        )
+
+    def spread_copy(flow, k):
+        return remote(
+            full.at[flow, k], full.at[flow, k], sem[2].at[flow, k], sem[3].at[flow, k], {"tensor": roles[flow][2]}
+        )
+
+    @pl.loop(0, count + 2 * LAG * (size - 1))
+    def _(step):
+        for flow, (place, _, _) in enumerate(roles):
+            k = step - LAG * (size - 1 - place)
+            inside = both(k >= 0, k < count)
+
+            @pl.when(both(inside, place > 0, place < size - 1))
+            def _(flow=flow, k=k):
+                reduce_copy(flow, k, sums).wait_recv()
+                sums[flow, k] = (slots[flow, k].astype(F32) + part[flow, k].astype(F32)).astype(BF16)
+                reduce_copy(flow, k, sums).start()
+
+            @pl.when(both(inside, place == 0))
+            def _(flow=flow, k=k):
+                reduce_copy(flow, k, sums).wait_recv()
+                full[flow, k] = finish(flow, k, slots[flow, k].astype(F32) + part[flow, k].astype(F32))
+                spread_copy(flow, k).start()
+
+        for flow, (place, _, _) in enumerate(roles):
+            k = step - LAG * (size - 1) - LAG * place
+            inside = both(k >= 0, k < count, place > 0)
+
+            @pl.when(inside)
+            def _(flow=flow, k=k):
+                spread_copy(flow, k).wait_recv()
+
+            @pl.when(both(inside, place < size - 1))
+            def _(flow=flow, k=k):
+                spread_copy(flow, k).start()
+
+    for flow, (place, _, _) in enumerate(roles):
+
+        @pl.when(place > 0)
+        def _(flow=flow):
+            @pl.loop(0, count)
+            def _(k):
+                reduce_copy(flow, k, sums).wait_send()
+
+        @pl.when(place < size - 1)
+        def _(flow=flow):
+            @pl.loop(0, count)
+            def _(k):
+                spread_copy(flow, k).wait_send()
+
+
+def spread_start(size, mine, full, sem):
+    for flow, (place, _, away) in enumerate(line_roles(size)):
+
+        @pl.when(place == 0)
+        def _(flow=flow, away=away):
+            @pl.loop(0, mine.shape[0])
+            def _(k):
+                remote(
+                    mine.at[k], full.at[flow, k], sem[0].at[flow, k], sem[1].at[flow, k], {"tensor": away}
+                ).start()
+                full[flow, k] = mine[k]
+
+
+def spread_run(size, mine, full, sem):
+    count = mine.shape[0]
+    roles = line_roles(size)
+
+    def pass_on(flow, k):
+        return remote(
+            full.at[flow, k], full.at[flow, k], sem[0].at[flow, k], sem[1].at[flow, k], {"tensor": roles[flow][2]}
+        )
+
+    @pl.loop(0, count + LAG * (size - 1))
+    def _(step):
+        for flow, (place, _, _) in enumerate(roles):
+            k = step - LAG * place
+            inside = both(k >= 0, k < count, place > 0)
+
+            @pl.when(inside)
+            def _(flow=flow, k=k):
+                pass_on(flow, k).wait_recv()
+
+            @pl.when(both(inside, place < size - 1))
+            def _(flow=flow, k=k):
+                pass_on(flow, k).start()
+
+    for flow, (place, _, _) in enumerate(roles):
+
+        @pl.when(place < size - 1)
+        def _(flow=flow):
+            @pl.loop(0, count)
+            def _(k):
+                pass_on(flow, k).wait_send()
+
+
+def line_sems(count, kinds):
+    return [DMA((2, count))] * kinds
+
+
+def ctx_sum_kernel(sizes, part_ref, mine, total_ref, full, slots, *sem):
     me = lax.axis_index("ctx")
+    size = sizes["tensor"]
     peers = peers_of("ctx", sizes["ctx"])
-    greet([peers])
+    greet_line(size, [peers])
     copies = send_all(lambda other: (part_ref.at[other], slots.at[me]), peers, sem[0], sem[1])
+    spread_start(size, mine, full, sem[2:4])
     slots[me] = part_ref[me]
+    spread_run(size, mine, full, sem[2:4])
     wait_all(copies)
     total_ref[...] = slot_sum(slots, sizes["ctx"])
 
 
-def scatter_start(sizes, part_ref, slots, sem):
-    me = lax.axis_index("tensor")
-    peers = peers_of("tensor", sizes["tensor"])
-    copies = send_all(lambda other: (part_ref.at[other], slots.at[me]), peers, sem[0], sem[1])
-    slots[me] = part_ref[me]
-    return copies
-
-
-def spread_start(sizes, full_ref, value, sem):
-    me = lax.axis_index("tensor")
-    peers = peers_of("tensor", sizes["tensor"])
-    full_ref[me] = value
-    return send_all(lambda other: (full_ref.at[me], full_ref.at[me]), peers, sem[0], sem[1])
-
-
 def first_kernel(
-    sizes, part, tokens, bias, gain, shift, up, down,
+    sizes, part, tokens, fixed, up, down,
     full, out_ref, normed_ref, inverse_ref, wide_up, wide_down,
-    slots, *sem
+    slots, sums, *sem
 ):
-    me = lax.axis_index("tensor")
+    size, data = sizes["tensor"], sizes["dp"]
     mine = lax.axis_index("dp")
-    others = peers_of("dp", sizes["dp"])
-    greet([peers_of("tensor", sizes["tensor"]), others])
-    scatter = scatter_start(sizes, part, slots, sem[0:2])
-    ups = send_all(lambda other: (up, wide_up.at[mine]), others, sem[4], sem[5])
-    downs = send_all(lambda other: (down, wide_down.at[mine]), others, sem[6], sem[7])
+    greet_line(size, [pair_group(data)])
+    line_start(size, part, slots, sem[0:2])
+    place_up, place_down = (lambda index: wide_up.at[index]), (lambda index: wide_down.at[index])
+    ups = gather_start(data, up, place_up, sem[4:10])
+    downs = gather_start(data, down, place_down, sem[10:16])
     wide_up[mine] = up[...]
     wide_down[mine] = down[...]
-    wait_all(scatter)
-    first_sum = tokens[me].astype(F32) + slot_sum(slots, sizes["tensor"]) + bias[...]
-    first_out, normed, inverse = layer_norm(first_sum, gain[...], shift[...])
-    spread = spread_start(sizes, full, first_out.astype(BF16), sem[2:4])
-    out_ref[...] = first_out
-    normed_ref[...] = normed
-    inverse_ref[...] = inverse
+
+    def finish(flow, k, total):
+        first_sum = tokens[flow, k].astype(F32) + total + fixed[0:1]
+        first_out, normed, inverse = layer_norm(first_sum, fixed[1:2], fixed[2:3])
+        out_ref[k] = first_out
+        normed_ref[k] = normed
+        inverse_ref[k] = inverse
+        return first_out.astype(BF16)
+
+    line_run(size, part, slots, sums, full, sem[0:4], finish)
+    ups = gather_pass(data, ups, place_up, sem[4:10])
+    downs = gather_pass(data, downs, place_down, sem[10:16])
     wait_all(ups)
     wait_all(downs)
-    wait_all(spread)
+
+
+def add_row(vector_ref, index, value):
+    vector_ref[index : index + 1] += jnp.sum(value, axis=0, keepdims=True)
 
 
 def second_kernel(
-    sizes, part, first_out, cotangent, bias, gain, shift,
+    sizes, part, first_out, cotangent, fixed,
     full, output_ref, back_ref, vector_ref,
-    slots, *sem
+    slots, sums, *sem
 ):
-    me = lax.axis_index("tensor")
-    greet([peers_of("tensor", sizes["tensor"])])
-    scatter = scatter_start(sizes, part, slots, sem[0:2])
-    wait_all(scatter)
-    second_sum = first_out[...] + slot_sum(slots, sizes["tensor"]) + bias[...]
-    result, normed, inverse = layer_norm(second_sum, gain[...], shift[...])
-    upstream = cotangent[me].astype(F32)
-    d_second = norm_back(upstream, normed, inverse, gain[...])
-    spread = spread_start(sizes, full, d_second.astype(BF16), sem[2:4])
-    output_ref[...] = result.astype(BF16)
-    back_ref[...] = d_second
-    vector_ref[0:1] = jnp.sum(upstream, axis=0, keepdims=True)
-    vector_ref[1:2] = jnp.sum(upstream * normed, axis=0, keepdims=True)
-    vector_ref[2:3] = jnp.sum(d_second, axis=0, keepdims=True)
-    wait_all(spread)
-
-
-def grads_start(sizes, grads, slots, sem):
-    mine = lax.axis_index("dp")
-    others = peers_of("dp", sizes["dp"])
-    copies = send_all(lambda other: (grads.at[other], slots.at[mine]), others, sem[0], sem[1])
-    slots[mine] = grads[mine]
+    size = sizes["tensor"]
+    greet_line(size, [])
+    line_start(size, part, slots, sem[0:2])
+    vector_ref[...] = jnp.zeros_like(vector_ref)
+
+    def finish(flow, k, total):
+        second_sum = first_out[k] + total + fixed[3:4]
+        result, normed, inverse = layer_norm(second_sum, fixed[4:5], fixed[5:6])
+        upstream = cotangent[flow, k].astype(F32)
+        d_second = norm_back(upstream, normed, inverse, fixed[4:5])
+        output_ref[k] = result.astype(BF16)
+        back_ref[k] = d_second
+        add_row(vector_ref, 0, upstream)
+        add_row(vector_ref, 1, upstream * normed)
+        add_row(vector_ref, 2, d_second)
+        return d_second.astype(BF16)
+
+    line_run(size, part, slots, sums, full, sem[0:4], finish)
+
+
+def grads_start(size, grads, chip, sem):
+    me, partner, _ = pair_roles(size)
+    copy = remote(
+        grads.at[:, lax.rem(partner, 2)], chip, sem[0].at[0], sem[1].at[0], {"dp": partner}
+    )
+    copy.start()
+    return copy
+
+
+def grads_far(size, copy, grads, chip, merged, slots, sem):
+    me, _, far = pair_roles(size)
+    copy.wait()
+    merged[...] = (grads[:, lax.rem(me, 2)].astype(F32) + chip[...].astype(F32)).astype(BF16)
+    copies = [
+        remote(
+            merged.at[lax.div(to, 2)], slots.at[lax.div(me, 2)], sem[2].at[step], sem[3].at[step], {"dp": to}
+        )
+        for step, (to, _) in enumerate(far)
+    ]
+    for moving in copies:
+        moving.start()
+    slots[lax.div(me, 2)] = merged[lax.div(me, 2)]
     return copies
 
 
-def grads_middle(sizes, copies, slots, blocks, sem):
-    wait_all(copies)
+def blocks_start(sizes, value, blocks, sem):
     me = lax.axis_index("ctx")
-    blocks[me] = slot_sum(slots, sizes["dp"]).astype(BF16)
+    blocks[me] = value
     return send_all(
         lambda other: (blocks.at[me], blocks.at[me]), peers_of("ctx", sizes["ctx"]), sem[0], sem[1]
     )
 
 
 def third_kernel(
-    sizes, part, d_second, normed_ref, inverse_ref, gain, grads_a, grads_b,
-    full, back_ref, vector_ref, owned_a, owned_b,
-    slots, slots_a, slots_b, blocks_a, blocks_b, *sem
+    sizes, part, d_second, normed_ref, inverse_ref, fixed, grads_a, grads_b,
+    full, back_ref, vector_ref, block_a, block_b,
+    slots, sums, chip_a, chip_b, merged_a, merged_b, far_a, far_b, *sem
 ):
-    greet(
-        [
-            peers_of("tensor", sizes["tensor"]),
-            peers_of("dp", sizes["dp"]),
-            peers_of("ctx", sizes["ctx"]),
-        ]
-    )
-    scatter = scatter_start(sizes, part, slots, sem[0:2])
-    moving_a = grads_start(sizes, grads_a, slots_a, sem[4:6])
-    moving_b = grads_start(sizes, grads_b, slots_b, sem[6:8])
-    wait_all(scatter)
-    d_first = slot_sum(slots, sizes["tensor"]) + d_second[...]
-    normed = normed_ref[...]
-    d_attn = norm_back(d_first, normed, inverse_ref[...], gain[...])
-    spread = spread_start(sizes, full, d_attn.astype(BF16), sem[2:4])
-    back_ref[...] = d_attn
-    vector_ref[0:1] = jnp.sum(d_first, axis=0, keepdims=True)
-    vector_ref[1:2] = jnp.sum(d_first * normed, axis=0, keepdims=True)
-    vector_ref[2:3] = jnp.sum(d_attn, axis=0, keepdims=True)
-    moving_a = grads_middle(sizes, moving_a, slots_a, blocks_a, sem[8:10])
-    moving_b = grads_middle(sizes, moving_b, slots_b, blocks_b, sem[10:12])
+    size, data = sizes["tensor"], sizes["dp"]
+    greet_line(size, [pair_group(data)])
+    line_start(size, part, slots, sem[0:2])
+    near_a = grads_start(data, grads_a, chip_a, sem[4:8])
+    near_b = grads_start(data, grads_b, chip_b, sem[8:12])
+    vector_ref[...] = jnp.zeros_like(vector_ref)
+    moving_a = grads_far(data, near_a, grads_a, chip_a, merged_a, far_a, sem[4:8])
+    moving_b = grads_far(data, near_b, grads_b, chip_b, merged_b, far_b, sem[8:12])
+
+    def finish(flow, k, total):
+        d_first = total + d_second[k]
+        normed = normed_ref[k]
+        d_attn = norm_back(d_first, normed, inverse_ref[k], fixed[1:2])
+        back_ref[k] = d_attn
+        add_row(vector_ref, 0, d_first)
+        add_row(vector_ref, 1, d_first * normed)
+        add_row(vector_ref, 2, d_attn)
+        return d_attn.astype(BF16)
+
+    line_run(size, part, slots, sums, full, sem[0:4], finish)
+    wait_all(moving_a)
+    block_a[...] = slot_sum(far_a, data // 2).astype(BF16)
+    wait_all(moving_b)
+    block_b[...] = slot_sum(far_b, data // 2).astype(BF16)
+
+
+def last_kernel(
+    sizes, part, d_attn, grads, block_a, block_b, vectors,
+    full, owned, owned_a, owned_b, vector_ref,
+    slots, sums, chip, merged, far, blocks, blocks_a, blocks_b, slots_v, grid_v, *sem
+):
+    size, data = sizes["tensor"], sizes["dp"]
+    me = lax.axis_index("tensor")
+    rows = peers_of("tensor", size)
+    here, everyone = grid_peers(sizes)
+    greet([rows, everyone])
+    line_start(size, part, slots, sem[0:2])
+    small = send_all(lambda other: (vectors, slots_v.at[me]), rows, sem[8], sem[9])
+    near = grads_start(data, grads, chip, sem[4:8])
+    moving_a = blocks_start(sizes, block_a[...], blocks_a, sem[12:14])
+    moving_b = blocks_start(sizes, block_b[...], blocks_b, sem[14:16])
+    slots_v[me] = vectors[...]
+    moving = grads_far(data, near, grads, chip, merged, far, sem[4:8])
+    wait_all(small)
+    own = vectors[...]
+    row_ids = lax.broadcasted_iota(jnp.int32, own.shape, 0)
+    grid_v[here] = jnp.where(row_ids < 6, slot_sum(slots_v, size), own)
+    small = send_all(lambda other: (grid_v.at[here], grid_v.at[here]), everyone, sem[10], sem[11])
+
+    def finish(flow, k, total):
+        return (total + d_attn[k]).astype(BF16)
+
+    line_run(size, part, slots, sums, full, sem[0:4], finish)
+    wait_all(moving)
+    moving = blocks_start(sizes, slot_sum(far, data // 2).astype(BF16), blocks, sem[16:18])
+    wait_all(small)
+    vector_ref[...] = slot_sum(grid_v, data * sizes["ctx"])
     wait_all(moving_a)
     owned_a[...] = slot_sum(blocks_a, sizes["ctx"])
     wait_all(moving_b)
     owned_b[...] = slot_sum(blocks_b, sizes["ctx"])
-    wait_all(spread)
-
-
-def last_kernel(
-    sizes, part, d_attn, grads, vectors,
-    full, owned, vector_ref,
-    slots, slots_g, blocks, slots_v, grid_v, *sem
-):
-    me = lax.axis_index("tensor")
-    rows = peers_of("tensor", sizes["tensor"])
-    here, everyone = grid_peers(sizes)
-    greet([rows, everyone])
-    small = send_all(lambda other: (vectors, slots_v.at[me]), rows, sem[8], sem[9])
-    slots_v[me] = vectors[...]
-    scatter = scatter_start(sizes, part, slots, sem[0:2])
-    moving = grads_start(sizes, grads, slots_g, sem[4:6])
-    wait_all(small)
-    own = vectors[...]
-    row_ids = lax.broadcasted_iota(jnp.int32, own.shape, 0)
-    grid_v[here] = jnp.where(row_ids < 6, slot_sum(slots_v, sizes["tensor"]), own)
-    small = send_all(lambda other: (grid_v.at[here], grid_v.at[here]), everyone, sem[10], sem[11])
-    wait_all(scatter)
-    d_tokens = slot_sum(slots, sizes["tensor"]) + d_attn[...]
-    spread = spread_start(sizes, full, d_tokens.astype(BF16), sem[2:4])
-    moving = grads_middle(sizes, moving, slots_g, blocks, sem[6:8])
-    wait_all(small)
-    vector_ref[...] = slot_sum(grid_v, sizes["dp"] * sizes["ctx"])
     wait_all(moving)
     owned[...] = slot_sum(blocks, sizes["ctx"])
-    wait_all(spread)
 
 
 CONTRACT_LAST = (((1,), (1,)), ((), ()))
@@ -399,39 +626,41 @@
     data, blocks, ranks = sizes["dp"], sizes["ctx"], sizes["tensor"]
     rows_in = tokens[0]
     row_count, model = rows_in.shape
-    part_rows = row_count // ranks
+    half = row_count // 2
+    chunk = math.gcd(half, 32)
+    chunks = half // chunk
     piece, local_width = qkv_weight.shape[1:]
     up_width = up_weight.shape[1]
     score_scale = 1.0 / math.sqrt(HD)
-    split = (ranks, part_rows, model)
-    part_slots = pltpu.VMEM(split, BF16)
-    local = shaped((part_rows, model), F32)
-    row = lambda vector: vector[None]
-
-    wide_qkv, wide_proj = call(
+    split = (2, chunks, chunk, model)
+    line_scratch = [pltpu.VMEM(split, BF16)] * 2 + line_sems(chunks, 4)
+    local = shaped(split[1:], F32)
+    fixed = jnp.stack([proj_bias, first_gain, first_shift, down_bias, second_gain, second_shift])
+
+    (wide_qkv,) = call(
         functools.partial(gather_kernel, sizes),
-        [shaped((3, data, piece, local_width), BF16), shaped((data,) + proj_weight.shape, BF16)],
-        sems(data - 1) * 2,
+        [shaped((3, data, piece, local_width), BF16)],
+        pair_sems(data),
         0,
-        (qkv_weight, proj_weight),
+        (qkv_weight,),
         "gather_weights",
     )
     wide_qkv = wide_qkv.reshape(3, model, local_width)
-    wide_proj = wide_proj.transpose(1, 0, 2).reshape(local_width, model)
 
     projected = jnp.einsum("td,ide->ite", rows_in, wide_qkv, preferred_element_type=F32)
     queries = (projected[0] + query_bias).astype(BF16)
     own_kv = jnp.concatenate(
         [projected[1].astype(BF16), (projected[2] + value_bias).astype(BF16)], axis=1
     )
-    (kv,) = call(
+    kv, wide_proj = call(
         functools.partial(ctx_gather_kernel, sizes),
-        [shaped((blocks,) + own_kv.shape, BF16)],
-        sems(blocks - 1),
+        [shaped((blocks,) + own_kv.shape, BF16), shaped((data,) + proj_weight.shape, BF16)],
+        sems(blocks - 1) + pair_sems(data),
         1,
-        (own_kv,),
+        (own_kv, proj_weight),
         "gather_keys",
     )
+    wide_proj = wide_proj.transpose(1, 0, 2).reshape(local_width, model)
     kv = kv.reshape(blocks * row_count, 2 * local_width)
     keys, values = kv[:, :local_width], kv[:, local_width:]
     attended, attended_low, log_total = attention_call(
@@ -452,18 +681,16 @@
             shaped(split, BF16),
             local,
             local,
-            shaped((part_rows, 1), F32),
+            shaped((chunks, chunk, 1), F32),
             shaped((data,) + up_weight.shape, BF16),
             shaped((data,) + down_weight.shape, BF16),
         ],
-        [part_slots] + sems(ranks - 1) * 2 + sems(data - 1) * 2,
+        line_scratch + pair_sems(data) * 2,
         2,
         (
             attn_part.reshape(split),
             rows_in.reshape(split),
-            row(proj_bias),
-            row(first_gain),
-            row(first_shift),
+            fixed,
             up_weight,
             down_weight,
         ),
@@ -478,20 +705,17 @@
     down_part = jnp.dot(hidden, wide_down, preferred_element_type=F32).astype(BF16)
     d_second_low, output_part, d_second, second_vectors = call(
         functools.partial(second_kernel, sizes),
-        [shaped(split, BF16), shaped((part_rows, model), BF16), local, shaped((3, model), F32)],
-        [part_slots] + sems(ranks - 1) * 2,
+        [shaped(split, BF16), shaped(split[1:], BF16), local, shaped((3, model), F32)],
+        line_scratch,
         3,
         (
             down_part.reshape(split),
             first_out,
             cotangent[0].reshape(split),
-            row(down_bias),
-            row(second_gain),
-            row(second_shift),
+            fixed,
         ),
         "second_norm",
     )
-    output = lax.all_gather(output_part, "tensor", axis=0, tiled=True)[None]
     d_second_low = d_second_low.reshape(row_count, model)
     grad_down = jnp.einsum("td,tf->df", d_second_low, hidden, preferred_element_type=F32)
     d_hidden = jnp.einsum("td,fd->tf", d_second_low, wide_down, preferred_element_type=F32)
@@ -502,24 +726,22 @@
     first_part = jnp.einsum("tf,df->td", d_pre_low, wide_up, preferred_element_type=F32).astype(BF16)
 
     grad_shape = (data, model // data, up_width)
-    grad_slots = pltpu.VMEM(grad_shape, BF16)
-    ctx_slots = pltpu.VMEM((blocks,) + grad_shape[1:], BF16)
-    d_attn_low, d_attn, first_vectors, own_up, own_down = call(
+    paired = (data // 2, 2) + grad_shape[1:]
+    pair_slots = pltpu.VMEM((data // 2,) + grad_shape[1:], BF16)
+    pair_moves = sems(1) + sems(max(1, data // 2 - 1))
+    d_attn_low, d_attn, first_vectors, block_up, block_down = call(
         functools.partial(third_kernel, sizes),
-        [shaped(split, BF16), local, shaped((3, model), F32)] + [shaped(grad_shape[1:], F32)] * 2,
-        [part_slots, grad_slots, grad_slots, ctx_slots, ctx_slots]
-        + sems(ranks - 1) * 2
-        + sems(data - 1) * 2
-        + sems(blocks - 1) * 2,
+        [shaped(split, BF16), local, shaped((3, model), F32)] + [shaped(grad_shape[1:], BF16)] * 2,
+        line_scratch[:2] + [pair_slots] * 6 + line_scratch[2:] + pair_moves * 2,
         4,
         (
             first_part.reshape(split),
             d_second,
             first_normed,
             first_inverse,
-            row(first_gain),
-            grad_up.astype(BF16).reshape(grad_shape),
-            grad_down.astype(BF16).reshape(grad_shape),
+            fixed,
+            grad_up.astype(BF16).reshape(paired),
+            grad_down.astype(BF16).reshape(paired),
         ),
         "first_norm_back",
     )
@@ -534,12 +756,12 @@
     )
     kv_part = jnp.concatenate([key_grads.astype(BF16), value_grads.astype(BF16)], axis=1)
     kv_shape = (blocks, row_count, 2 * local_width)
-    (own_grads,) = call(
+    own_grads, output = call(
         functools.partial(ctx_sum_kernel, sizes),
-        [shaped(kv_shape[1:], F32)],
-        [pltpu.VMEM(kv_shape, BF16)] + sems(blocks - 1),
+        [shaped(kv_shape[1:], F32), shaped(split, BF16)],
+        [pltpu.VMEM(kv_shape, BF16)] + sems(blocks - 1) + line_sems(chunks, 2),
         5,
-        (kv_part.reshape(kv_shape),),
+        (kv_part.reshape(kv_shape), output_part),
         "sum_keys",
     )
     grad_query_bias = jnp.sum(d_query, axis=0)
@@ -550,7 +772,8 @@
     flat_qkv = wide_qkv.transpose(1, 0, 2).reshape(model, 3 * local_width)
     input_part = jnp.einsum("te,de->td", d_stack, flat_qkv, preferred_element_type=F32).astype(BF16)
 
-    last_shape = (data, model // data, 4 * local_width)
+    last_shape = (data // 2, 2, model // data, 4 * local_width)
+    last_pair = pltpu.VMEM((data // 2,) + last_shape[2:], BF16)
     last_grads = jnp.concatenate([grad_qkv.astype(BF16), grad_proj.astype(BF16)], axis=1)
     vector_width = max(model, up_width, 2 * local_width)
     pad = lambda array: jnp.pad(array, ((0, 0), (0, vector_width - array.shape[1])))
@@ -562,29 +785,39 @@
             pad(jnp.concatenate([grad_query_bias, grad_value_bias])[None]),
         ]
     )
-    grad_tokens, own_last, sums = call(
+    grad_tokens, own_last, own_up, own_down, sums = call(
         functools.partial(last_kernel, sizes),
-        [shaped(split, BF16), shaped(last_shape[1:], F32), shaped(vectors.shape, F32)],
-        [
-            part_slots,
-            pltpu.VMEM(last_shape, BF16),
-            pltpu.VMEM((blocks,) + last_shape[1:], BF16),
+        [shaped(split, BF16), shaped(last_shape[2:], F32)]
+        + [shaped(grad_shape[1:], F32)] * 2
+        + [shaped(vectors.shape, F32)],
+        line_scratch[:2]
+        + [last_pair] * 3
+        + [pltpu.VMEM((blocks,) + last_shape[2:], BF16)]
+        + [pltpu.VMEM((blocks,) + grad_shape[1:], BF16)] * 2
+        + [
             pltpu.VMEM((ranks,) + vectors.shape, F32),
             pltpu.VMEM((data * blocks,) + vectors.shape, F32),
         ]
-        + sems(ranks - 1) * 2
-        + sems(data - 1)
-        + sems(blocks - 1)
+        + line_scratch[2:]
+        + pair_moves
         + sems(ranks - 1)
-        + sems(data * blocks - 1),
+        + sems(data * blocks - 1)
+        + sems(blocks - 1) * 3,
         6,
-        (input_part.reshape(split), d_attn, last_grads.reshape(last_shape), vectors),
+        (
+            input_part.reshape(split),
+            d_attn,
+            last_grads.reshape(last_shape),
+            block_up,
+            block_down,
+            vectors,
+        ),
         "token_grads",
     )
     grad_tokens = grad_tokens.reshape(1, row_count, model).astype(F32)
     own_qkv = own_last[:, : 3 * local_width].reshape(-1, 3, local_width).transpose(1, 0, 2)
     return (
-        output,
+        output.reshape(1, row_count, model),
         grad_tokens,
         own_qkv,
         sums[7, :local_width],

time: 308 us -> 279 us (0.906)
  blocking collectives: 20.4 us -> 0 us
  Pallas kernels: 228 us -> 223 us
  local copies, waits for them, and re-layouts: 28.5 us -> 25.4 us
    all_gather x1 -> x0, blocking collectives: 20.4 us -> none  [per_device(): output = lax.all_gather(output_part, 'tensor', axis=0, tiled=True)[None]]
    broadcast_in_dim x6 -> x0, local copies, waits for them, and re-layouts: 7.6 us -> none  [per_device(): row = lambda vector: vector[None]]
    another operation x0 -> x7, local copies, waits for them, and re-layouts: none -> 4.77 us  [per_device(): jnp.stack([proj_bias, first_gain, first_shift, down_bias, second_gain, se...]
    pallas_call x7, Pallas kernels: 214 us -> 209 us  [call(): pl.pallas_call(kernel, out_shape=outs, in_specs=[VMEM_SPEC] * len(args),...]
    unnamed x44 -> x46, local copies, waits for them, and re-layouts: 6.57 us -> 6.51 us
where the time goes in v2:
time: 279 us; the launch traced here: 278 us
  Pallas kernels  223 us (80%)
  local copies, waits for them, and re-layouts  25.4 us (9%)
  matrix products  19.8 us (7%)
  other arithmetic  7.72 us (3%)
    pallas_call x7, Pallas kernels, call(): pl.pallas_call(kernel, out_shape=outs, in_specs=[VMEM_SPEC] * len(args),...  209 us
    pallas_call x2, Pallas kernels, attention_call(): pl.pallas_call(kernel, out_shape=outs, in_specs=[pl.BlockSpec(memory_spac...  14.2 us
    unnamed x46, local copies, waits for them, and re-layouts  6.51 us

profile of v2, /device:TPU:0, one launch (start us, length us, event | category | flops | bytes accessed | tf_op | source)
XLA Modules:
  0.0 278.0 jit_solution(2454263444213663736)
XLA Ops:
  6.1 1.9 copy.52.down
  8.0 14.0 %gather_weights.1 = bf16[3,4,192,192]{3,2,1,0:T(8,128)(2,1)} custom-call(bf16[3,192,192]{2,1,0:T(8,128)(2,1)} %qkv_ref.1), custom_call_target="tpu_custom_call" | custom-call | tf_op jit(solution)/shard_map/gather_weights/pallas_call | solution.py:116
  21.9 1.8 copy.55
  26.3 14.1 %gather_keys.1 = (bf16[2,512,384]{2,1,0:T(8,128)(2,1)}, bf16[4,192,192]{2,1,0:T(8,128)(2,1)}) custom-call(bf16[512,384]{1,0:T(8,128)(2,1)} %pad_maximum_fusion.5.own_ref, bf16[192,192]{1,0:T(8,128)(2,1)} %proj_ref.1), custom_call_target="tpu_custom_call" | custom-call | tf_op jit(solution)/shard_map/gather_keys/pallas_call | solution.py:116
  43.2 5.6 %attention_forward.1 = (f32[512,192]{1,0:T(8,128)}, bf16[512,192]{1,0:T(8,128)(2,1)}, f32[512,3]{1,0:T(8,128)}) custom-call(s32[1]{0:T(128)S(6)} %copy.65.length_ref, bf16[512,192]{1,0:T(8,128)(2,1)} %get-tuple-element.128.q_ref, bf16[1024,192]{1,0:T(8,128)(2,1)} %get-tuple-element.130.k_ref, bf16[1024,192]{1,0:T(8,128)(2,1)} %get-tuple-element.129.v_ref), custom_call_target="tpu_custom_call" | custom-call | tf_op jit(solution)/shard_map/attention_forward/pallas_call | solution.py:597
  48.9 2.2 convolution_convert_fusion.6
  51.1 39.2 %first_norm.1 = (bf16[2,8,32,768]{3,2,1,0:T(8,128)(2,1)}, f32[8,32,768]{2,1,0:T(8,128)}, f32[8,32,768]{2,1,0:T(8,128)}, f32[8,32,1]{2,1,0:T(8,128)}, bf16[4,192,...) custom-call(bf16[2,8,32,768]{3,2,1,0:T(8,128)(2,1)} %bitcast.83, bf16[2,8,32,768]{3,2,1,0:T(8,128)(2,1)} %bitcast.93, ...), custom_call_target="tpu_custom_call" | custom-call | tf_op jit(solution)/shard_map/first_norm/pallas_call | solution.py:116
  90.3 1.8 copy.53
  92.1 2.0 multiply_convert_fusion
  94.1 1.7 convolution_convert_fusion.4
  95.8 34.0 %second_norm.1 = (bf16[2,8,32,768]{3,2,1,0:T(8,128)(2,1)}, bf16[8,32,768]{2,1,0:T(8,128)(2,1)}, f32[8,32,768]{2,1,0:T(8,128)}, f32[3,768]{1,0:T(4,128)}) custom-call(bf16[2,8,32,768]{3,2,1,0:T(8,128)(2,1)} %bitcast.98, f32[8,32,768]{2,1,0:T(8,128)} %get-tuple-element.51.first_out, bf16[2,8,32,768]{3,2,1,0:T(8,128)(2,1)} %bitcast.95, f32[6,768]{1,0:T(8,128)} %stack.27.fixed), custom_call_target="tpu_custom_call" | custom-call | tf_op jit(solution)/shard_map/second_norm/pallas_call | solution.py:116
  129.9 2.3 fusion.20
  132.1 1.8 convolution_convert_fusion
  134.0 1.7 convolution_convert_fusion.3
  135.7 1.8 convolution_convert_fusion.1
  137.5 35.5 %first_norm_back.1 = (bf16[2,8,32,768]{3,2,1,0:T(8,128)(2,1)}, f32[8,32,768]{2,1,0:T(8,128)}, f32[3,768]{1,0:T(4,128)}, bf16[192,768]{1,0:T(8,128)(2,1)}, bf16[192,768]{1,0:T(8,128)(2,1)}) custom-call(bf16[2,8,32,768]{3,2,1,0:T(8,128)(2,1)} %bitcast.92, f32[8,32,768]{2,1,0:T(8,128)} %get-tuple-element.53.d_second, ...), custom_call_target="tpu_custom_call" | custom-call | tf_op jit(solution)/shard_map/first_norm_back/pallas_call | solution.py:116
  173.0 1.5 convolution_convert_fusion.8
  174.5 1.5 convolution_convert_fusion.7
  176.9 8.6 %attention_backward.1 = (f32[512,192]{1,0:T(8,128)}, f32[1024,192]{1,0:T(8,128)}, f32[1024,192]{1,0:T(8,128)}) custom-call(s32[1]{0:T(128)S(6)} %copy.65.length_ref, bf16[512,192]{1,0:T(8,128)(2,1)} %get-tuple-element.128.q_ref, bf16[1024,192]{1,0:T(8,128)(2,1)} %get-tuple-element.130.k_ref, bf16[1024,192]{1,0:T(8,128)(2,1)} %get-tuple-element.129.v_ref, ...), custom_call_target="tpu_custom_call" | custom-call | tf_op jit(solution)/shard_map/attention_backward/pallas_call | solution.py:597
  188.3 22.4 %sum_keys.1 = (f32[512,384]{1,0:T(8,128)}, bf16[2,8,32,768]{3,2,1,0:T(8,128)(2,1)}) custom-call(bf16[2,512,384]{2,1,0:T(8,128)(2,1)} %bitcast.80, bf16[8,32,768]{2,1,0:T(8,128)(2,1)} %get-tuple-element.61.mine), custom_call_target="tpu_custom_call" | custom-call | tf_op jit(solution)/shard_map/sum_keys/pallas_call | solution.py:116
  212.9 1.7 convolution_convert_fusion.5
  215.5 1.5 copy.56
  217.0 50.0 %token_grads.1 = (bf16[2,8,32,768]{3,2,1,0:T(8,128)(2,1)}, f32[192,768]{1,0:T(8,128)}, f32[192,768]{1,0:T(8,128)}, f32[192,768]{1,0:T(8,128)}, f32[8,768]{1,0:T(8,128)}) custom-call(bf16[2,8,32,768]{3,2,1,0:T(8,128)(2,1)} %bitcast.97, f32[8,32,768]{2,1,0:T(8,128)} %get-tuple-element.65.d_attn, bf16[2,2,192,768]{3,2,1,0:T(8,128)(2,1)} %bitcast.77, ...), custom_call_target="tpu_custom_call" | custom-call | tf_op jit(solution)/shard_map/token_grads/pallas_call | solution.py:116
  268.4 1.7 slice_reduce_fusion.1
  (76 shorter events, 26.3 us)
Async XLA Ops:
  7.9 15.7 %copy-start.5 = (bf16[1,512,768]{2,1,0:T(8,128)(2,1)S(1)}, bf16[1,512,768]{2,1,0:T(8,128)(2,1)}, u32[]{:S(2)}) copy-start(bf16[1,512,768]{2,1,0:T(8,128)(2,1)} %param.16) | copy-start | bytes 2359300
  21.9 1.8 copy-start
  23.7 0.8 copy-start.14
  23.7 0.8 copy-start.15
  40.3 1.7 copy-start.2
  90.3 1.8 copy-start.16
  90.3 1.8 copy-start.19
  129.9 2.3 copy-start.18
  134.0 1.7 copy-start.17
  137.5 37.0 %copy-start.4 = (bf16[512,192]{1,0:T(8,128)(2,1)S(1)}, bf16[512,192]{1,0:T(8,128)(2,1)}, u32[]{:S(2)}) copy-start(bf16[512,192]{1,0:T(8,128)(2,1)} %get-tuple-element.46) | copy-start | bytes 589828
  185.5 1.5 copy-start.3
  187.1 23.7 %copy-start.11 = (f32[512,192]{1,0:T(8,128)S(1)}, f32[512,192]{1,0:T(8,128)}, u32[]{:S(2)}) copy-start(f32[512,192]{1,0:T(8,128)} %get-tuple-element.63) | copy-start | bytes 1179652
  188.3 23.9 %copy-start.12 = (f32[3,768]{1,0:T(4,128)S(1)}, f32[3,768]{1,0:T(4,128)}, u32[]{:S(2)}) copy-start(f32[3,768]{1,0:T(4,128)} %get-tuple-element.68) | copy-start | bytes 27652
  188.3 23.9 %copy-start.13 = (f32[3,768]{1,0:T(4,128)S(1)}, f32[3,768]{1,0:T(4,128)}, u32[]{:S(2)}) copy-start(f32[3,768]{1,0:T(4,128)} %get-tuple-element.69) | copy-start | bytes 27652
  210.7 2.1 copy-start.1
  212.9 1.7 copy-start.6
  272.1 2.1 copy-start.8
  273.2 2.3 copy-start.7
  274.2 2.1 copy-start.10
  275.5 1.7 copy-start.9
